TPU v7x, 32 devices: a whole 2x2x4 slice. The times are simulated.
32 devices in a mesh: row: 4 (over y, core), col: 8 (over z, x).
Axes of the slice: x: 2, y: 2, z: 4, core: 2. Of those that a mesh axis runs over, the one named last changes fastest.
Arguments:
- coords: float32 [64, 16384], P(None, ('row', 'col')), may hold values from -6 to 6
- dissimilarity: float32 [16384, 8192], P('row', 'col'), as said below
Outputs:
- updated: float32 [64, 16384], P(None, ('row', 'col'))
Inputs may be any that keep to these rules, and one draw needn't show every extreme that they name: `dissimilarity`: each unordered pair of distinct samples appears in exactly one entry, placed as the steps state; the entries that name no pair are positive too.
All inputs are finite; a program needn't handle non-finite values.
Results may differ from a plain program's by a relative error of at most 0.0003.
Values sent between devices are 32-bit elements; how exact they have to be, the bound alone decides.
A program may use at most 128 MiB of HBM per device.

v0:
```python
import jax
import jax.numpy as jnp
from jax import lax
from jax.sharding import PartitionSpec as P

ITERS = 2


def from_root(value, axis, source):
    kept = jnp.where(lax.axis_index(axis) == source, value, 0).astype(value.dtype)
    return lax.psum(kept, axis)


def compute_ratios(values, leading, trailing):
    inner_prod = lax.dot_general(
        leading,
        trailing,
        (((0,), (0,)), ((), ())),
        precision=lax.Precision.HIGHEST,
        preferred_element_type=jnp.float32,
    )
    leading_norms = jnp.sum(leading * leading, axis=0)
    trailing_norms = jnp.sum(trailing * trailing, axis=0)
    spacing = jnp.sqrt(leading_norms[:, None] + trailing_norms[None, :] - 2.0 * inner_prod + 1.0)
    return values / spacing


def pair_terms(leading, trailing, ratios):
    pulled = lax.dot_general(
        trailing,
        ratios,
        (((1,), (1,)), ((), ())),
        precision=lax.Precision.HIGHEST,
        preferred_element_type=jnp.float32,
    )
    pushed = lax.dot_general(
        leading,
        ratios,
        (((1,), (0,)), ((), ())),
        precision=lax.Precision.HIGHEST,
        preferred_element_type=jnp.float32,
    )
    leading_terms = leading * jnp.sum(ratios, axis=1)[None, :] - pulled
    trailing_terms = trailing * jnp.sum(ratios, axis=0)[None, :] - pushed
    return (leading_terms, trailing_terms)


def offdiagonal_terms(values, rows_coords, cols_coords, row_first):
    half_width = values.shape[1]
    leading = jnp.where(row_first, rows_coords, cols_coords)
    partner = jnp.where(row_first, cols_coords, rows_coords)
    offset = jnp.where(row_first, 0, half_width).astype(jnp.int32)
    trailing = lax.dynamic_slice_in_dim(partner, offset, half_width, 1)
    ratios = compute_ratios(values, leading, trailing)
    leading_terms, trailing_terms = pair_terms(leading, trailing, ratios)
    placed = lax.dynamic_update_slice_in_dim(jnp.zeros_like(partner), trailing_terms, offset, 1)
    return (
        jnp.where(row_first, leading_terms, placed),
        jnp.where(row_first, placed, leading_terms),
    )


def diagonal_terms(values, rows_coords, cols_coords, row_first):
    half_width = values.shape[1]
    first_half = rows_coords[:, :half_width]
    second_half = rows_coords[:, half_width:]
    upper_values = values[:half_width]
    lower_values = values[half_width:]
    row_iota = lax.broadcasted_iota(jnp.int32, (half_width, half_width), 0)
    col_iota = lax.broadcasted_iota(jnp.int32, (half_width, half_width), 1)
    cross = compute_ratios(lower_values, second_half, first_half)
    cross_second, cross_first = pair_terms(second_half, first_half, cross)
    early = jnp.where(
        col_iota > row_iota, compute_ratios(upper_values, first_half, first_half), 0.0
    )
    late = jnp.where(
        col_iota < row_iota, compute_ratios(upper_values, second_half, second_half), 0.0
    )
    early_rows, early_cols = pair_terms(first_half, first_half, early)
    late_rows, late_cols = pair_terms(second_half, second_half, late)
    row_share = jnp.concatenate(
        [early_rows + early_cols + cross_first, late_rows + late_cols + cross_second], axis=1
    )
    return (row_share, jnp.zeros_like(row_share))


def tile_terms(values, rows_coords, cols_coords, row_index, col_index):
    return lax.cond(
        row_index == col_index,
        diagonal_terms,
        offdiagonal_terms,
        values,
        rows_coords,
        cols_coords,
        row_index < col_index,
    )


def local(coords, dissimilarity):
    half_width = dissimilarity.shape[1]
    block_width = 2 * half_width
    per_root = lax.axis_size("col") // lax.axis_size("row")
    tile_count = dissimilarity.shape[0] // block_width
    inverse_count = 1.0 / (block_width * lax.axis_size("col"))
    row_pos = lax.axis_index("row")
    col_pos = lax.axis_index("col")
    own_width = coords.shape[1]
    stacked_tiles = dissimilarity.reshape(tile_count, block_width, half_width)
    slot_indices = jnp.arange(tile_count, dtype=jnp.int32)
    column_offset = col_pos % per_root * block_width
    at_root = row_pos == col_pos // per_root
    rows_coords = lax.all_gather(coords, "col", axis=1, tiled=True)
    updated = coords
    for iteration in range(ITERS):
        root_piece = lax.dynamic_slice_in_dim(rows_coords, column_offset, block_width, 1)
        cols_coords = from_root(root_piece, "row", col_pos // per_root)

        def one_tile(partials, operands):
            row_part, col_part = partials
            values, slot_index = operands
            slot_start = slot_index * block_width
            tile_rows = lax.dynamic_slice_in_dim(rows_coords, slot_start, block_width, 1)
            row_share, col_share = tile_terms(
                values, tile_rows, cols_coords, row_pos * per_root + slot_index, col_pos
            )
            row_part = lax.dynamic_update_slice_in_dim(row_part, row_share, slot_start, 1)
            return ((row_part, col_part + col_share), None)

        initial = (jnp.zeros_like(rows_coords), jnp.zeros_like(cols_coords))
        (row_part, col_part), _ = lax.scan(one_tile, initial, (stacked_tiles, slot_indices))
        col_total = lax.psum(col_part, "row")
        placed = lax.dynamic_update_slice_in_dim(
            jnp.zeros_like(row_part), col_total, column_offset, 1
        )
        row_part = row_part + jnp.where(at_root, placed, 0.0)
        rows_coords = lax.psum(row_part, "col") * inverse_count
        updated = lax.dynamic_slice_in_dim(rows_coords, col_pos * own_width, own_width, 1)
    return updated


def solution(mesh):
    in_specs = (P(None, ("row", "col")), P("row", "col"))
    out_specs = P(None, ("row", "col"))
    return jax.shard_map(local, mesh=mesh, in_specs=in_specs, out_specs=out_specs, check_vma=False)
```

profile of v0, /device:TPU:14, one launch (start us, length us, event | category | flops | bytes accessed | tf_op | source)
XLA Modules:
  0.0 594.5 jit_solution(5631974758337346116)
XLA Ops:
  6.5 0.7 all-gather.2.cloned.1.call-update
  7.3 0.0 all-reduce.7.cloned.1.call-start
  7.3 41.5 %all-gather.2.cloned.1.call-done = f32[64,4096]{1,0:T(8,128)} async-done(((f32[64,512]{1,0:T(8,128)}), f32[64,4096]{1,0:T(8,128)}) %all-gather.2.cloned.1.call-update) | async-done | bytes 1048592 | tf_op jit(solution)/shard_map/all_gather | solution.py:112
  48.8 1.9 dynamic-slice_select_fusion.3
  50.7 0.0 all-reduce.9.cloned.1.call-start
  50.8 33.8 %all-reduce.7.cloned.1.call-done = f32[64,2048]{1,0:T(8,128)} async-done(((f32[64,2048]{1,0:T(8,128)}), f32[64,2048]{1,0:T(8,128)}) %all-reduce.7.cloned.1.call-update) | async-done | bytes 524304 | tf_op jit(solution)/shard_map/psum | solution.py:11
  84.6 0.1 broadcast.81.clone
  84.7 104.3 %while.38 = (s32[]{:T(128)}, f32[64,4096]{1,0:T(8,128)S(1)}, f32[64,2048]{1,0:T(8,128)S(1)}, s32[2]{0:T(128)S(1)}, s32[]{:T(128)}, /*index=5*/s32[]{:T(128)}, f3...) while((s32[]{:T(128)}, f32[64,4096]{1,0:T(8,128)S(1)}, ...), condition=%wide.region_16.17_spmd.clone, body=%wide.region_1.16_spmd.clone.sunk | while | flops 7275667456 | bytes 107037056 | solution.py:130
  84.8 0.7 dynamic_slice.84
  86.2 1.1 constant_dynamic-slice_fusion.4
  88.0 8.3 %dynamic-slice_bitcast_fusion.4 = f32[2048,1024]{1,0:T(8,128)} fusion(f32[2,2048,1024]{2,1,0:T(8,128)} %get-tuple-element.580, s32[]{:T(128)} %get-tuple-element.560), kind=kLoop, calls=%fused_computation.88.clone.1 | loop fusion | bytes 16777220 | tf_op jit(solution)/shard_map/while/body/jit(dynamic_index_in_dim)/squeeze | solution.py:130
  96.3 35.5 %conditional.6 = (f32[64,2048]{1,0:T(8,128)S(1)}, f32[64,2048]{1,0:T(8,128)S(1)}) conditional(s32[]{:T(128)} %convert_element_type.17, (s32[]{:T(128)}, s32[]{:T(128)}, f32[64,2048]{1,0:T(8,128)S(1)}, f32[64,2048]{1,0:T(8,128)S(1)}, f32[2048,1024]{1,0:T(8,128)}) %tuple.138, (f32[64,2048]{1,0:T(8,128)S(1)}, f32[2048,1024]{1,0:T(8,128)}) %tuple.106), branch_computations={%region_2.6_spmd, %region_7.15_spmd} | conditional | flops 7275405312 | bytes 84492352 | solution.py:88
  96.4 0.1 multiply_reduce_fusion
  96.5 11.8 %fusion.42 = (f32[1024]{0:T(1024)S(1)}, f32[2048]{0:T(1024)S(1)}, f32[2048,1024]{1,0:T(8,128)S(1)}) fusion(f32[2048,1024]{1,0:T(8,128)} %get-tuple-element.227, f32[64,2048]{1,0:T(8,128)S(1)} %get-tuple-element.390, f32[64,1024]{1,0:T(8,128)S(1)} %get-tuple-element.392, f32[1024]{0:T(1024)S(1)} %get-tuple-element.391, f32[2048]{0:T(1024)S(1)} %get-tuple-element.389), kind=kOutput, calls=%fused_computation.102 | convolution fusion | flops 1625289728 | bytes 17588224 | tf_op jit(solution)/shard_map/while/body/eval_jaxpr/cond/branch_0_fun/dot_general | solution.py:15
  108.3 5.2 fusion
  113.5 8.1 %broadcast_select_fusion.1 = (f32[64,2048]{1,0:T(8,128)S(1)}, f32[64,2048]{1,0:T(8,128)S(1)}) fusion(f32[64,2048]{1,0:T(8,128)S(1)} %fusion, pred[]{:T(512)S(6)} %lt.46, f32[64,1024]{1,0:T(8,128)S(1)} %get-tuple-element.392, f32[2048,1024]{1,0:T(8,128)S(1)} %get-tuple-element.405, f32[64,2048]{1,0:T(8,128)S(1)} %get-tuple-element.390, ...), kind=kOutput, calls=%fused_computation.8 | convolution fusion | flops 1611137024 | bytes 10756097 | tf_op jit(solution)/shard_map/while/body/eval_jaxpr/cond/branch_0_fun/dot_general | solution.py:29
  131.8 0.3 select_add_fusion.4
  136.2 0.7 dynamic_slice.84
  137.6 1.1 constant_dynamic-slice_fusion.4
  139.3 8.3 %dynamic-slice_bitcast_fusion.4 = f32[2048,1024]{1,0:T(8,128)} fusion(f32[2,2048,1024]{2,1,0:T(8,128)} %get-tuple-element.580, s32[]{:T(128)} %get-tuple-element.560), kind=kLoop, calls=%fused_computation.88.clone.1 | loop fusion | bytes 16777220 | tf_op jit(solution)/shard_map/while/body/jit(dynamic_index_in_dim)/squeeze | solution.py:130
  147.7 35.5 %conditional.6 = (f32[64,2048]{1,0:T(8,128)S(1)}, f32[64,2048]{1,0:T(8,128)S(1)}) conditional(s32[]{:T(128)} %convert_element_type.17, (s32[]{:T(128)}, s32[]{:T(128)}, f32[64,2048]{1,0:T(8,128)S(1)}, f32[64,2048]{1,0:T(8,128)S(1)}, f32[2048,1024]{1,0:T(8,128)}) %tuple.138, (f32[64,2048]{1,0:T(8,128)S(1)}, f32[2048,1024]{1,0:T(8,128)}) %tuple.106), branch_computations={%region_2.6_spmd, %region_7.15_spmd} | conditional | flops 7275405312 | bytes 84492352 | solution.py:88
  147.7 0.1 multiply_reduce_fusion
  147.8 12.0 %fusion.42 = (f32[1024]{0:T(1024)S(1)}, f32[2048]{0:T(1024)S(1)}, f32[2048,1024]{1,0:T(8,128)S(1)}) fusion(f32[2048,1024]{1,0:T(8,128)} %get-tuple-element.227, f32[64,2048]{1,0:T(8,128)S(1)} %get-tuple-element.390, f32[64,1024]{1,0:T(8,128)S(1)} %get-tuple-element.392, f32[1024]{0:T(1024)S(1)} %get-tuple-element.391, f32[2048]{0:T(1024)S(1)} %get-tuple-element.389), kind=kOutput, calls=%fused_computation.102 | convolution fusion | flops 1625289728 | bytes 17588224 | tf_op jit(solution)/shard_map/while/body/eval_jaxpr/cond/branch_0_fun/dot_general | solution.py:15
  159.9 5.2 fusion
  165.1 8.1 %broadcast_select_fusion.1 = (f32[64,2048]{1,0:T(8,128)S(1)}, f32[64,2048]{1,0:T(8,128)S(1)}) fusion(f32[64,2048]{1,0:T(8,128)S(1)} %fusion, pred[]{:T(512)S(6)} %lt.46, f32[64,1024]{1,0:T(8,128)S(1)} %get-tuple-element.392, f32[2048,1024]{1,0:T(8,128)S(1)} %get-tuple-element.405, f32[64,2048]{1,0:T(8,128)S(1)} %get-tuple-element.390, ...), kind=kOutput, calls=%fused_computation.8 | convolution fusion | flops 1611137024 | bytes 10756097 | tf_op jit(solution)/shard_map/while/body/eval_jaxpr/cond/branch_0_fun/dot_general | solution.py:29
  183.2 0.3 select_add_fusion.4
  189.0 0.8 copy-done.3
  189.8 0.0 all-reduce.11.cloned.1.call-start
  189.8 44.8 %all-reduce.9.cloned.1.call-done = f32[64,2048]{1,0:T(8,128)} async-done(((f32[64,2048]{1,0:T(8,128)}), f32[64,2048]{1,0:T(8,128)}) %all-reduce.9.cloned.1.call-update) | async-done | bytes 524304 | tf_op jit(solution)/shard_map/psum | solution.py:131
  234.7 0.1 add_dynamic-update-slice_fusion.1
  234.8 1.0 copy-done.5
  235.8 0.0 all-reduce.13.cloned.1.call-start
  235.9 80.8 %all-reduce.11.cloned.1.call-done = f32[64,4096]{1,0:T(8,128)} async-done(((f32[64,4096]{1,0:T(8,128)}), f32[64,4096]{1,0:T(8,128)}) %all-reduce.11.cloned.1.call-update) | async-done | bytes 1048592 | tf_op jit(solution)/shard_map/psum | solution.py:136
  316.7 2.4 broadcast_multiply_fusion
  319.1 1.9 dynamic-slice_select_fusion.2
  321.0 0.0 all-reduce.15.cloned.1.call-start
  321.0 32.8 %all-reduce.13.cloned.1.call-done = f32[64,2048]{1,0:T(8,128)} async-done(((f32[64,2048]{1,0:T(8,128)}), f32[64,2048]{1,0:T(8,128)}) %all-reduce.13.cloned.1.call-update) | async-done | bytes 524304 | tf_op jit(solution)/shard_map/psum | solution.py:11
  353.8 0.1 broadcast.81
  353.9 103.9 %while.39 = (s32[]{:T(128)}, f32[64,4096]{1,0:T(8,128)S(1)}, f32[64,2048]{1,0:T(8,128)S(1)}, s32[2]{0:T(128)S(1)}, s32[]{:T(128)}, /*index=5*/s32[]{:T(128)}, f3...) while((s32[]{:T(128)}, f32[64,4096]{1,0:T(8,128)S(1)}, ...), condition=%wide.region_35.36_spmd.clone, body=%wide.region_20.35_spmd.clone.sunk | while | flops 7275667456 | bytes 107037056 | solution.py:130
  354.1 0.7 dynamic_slice.87
  355.5 1.1 constant_dynamic-slice_fusion.5
  357.3 8.3 %dynamic-slice_bitcast_fusion.5 = f32[2048,1024]{1,0:T(8,128)} fusion(f32[2,2048,1024]{2,1,0:T(8,128)} %get-tuple-element.619, s32[]{:T(128)} %get-tuple-element.599), kind=kLoop, calls=%fused_computation.92.clone.1 | loop fusion | bytes 16777220 | tf_op jit(solution)/shard_map/while/body/jit(dynamic_index_in_dim)/squeeze | solution.py:130
  365.6 35.5 %conditional.7 = (f32[64,2048]{1,0:T(8,128)S(1)}, f32[64,2048]{1,0:T(8,128)S(1)}) conditional(s32[]{:T(128)} %convert_element_type.18, (s32[]{:T(128)}, s32[]{:T(128)}, f32[64,2048]{1,0:T(8,128)S(1)}, f32[64,2048]{1,0:T(8,128)S(1)}, f32[2048,1024]{1,0:T(8,128)}) %tuple.137, (f32[64,2048]{1,0:T(8,128)S(1)}, f32[2048,1024]{1,0:T(8,128)}) %tuple.110), branch_computations={%region_21.25_spmd, %region_26.34_spmd} | conditional | flops 7275405312 | bytes 84492352 | solution.py:88
  365.6 0.1 multiply_reduce_fusion.4
  365.7 11.8 %fusion.46 = (f32[1024]{0:T(1024)S(1)}, f32[2048]{0:T(1024)S(1)}, f32[2048,1024]{1,0:T(8,128)S(1)}) fusion(f32[2048,1024]{1,0:T(8,128)} %get-tuple-element.246, f32[64,2048]{1,0:T(8,128)S(1)} %get-tuple-element.394, f32[64,1024]{1,0:T(8,128)S(1)} %get-tuple-element.396, f32[1024]{0:T(1024)S(1)} %get-tuple-element.395, f32[2048]{0:T(1024)S(1)} %get-tuple-element.393), kind=kOutput, calls=%fused_computation.106 | convolution fusion | flops 1625289728 | bytes 17588224 | tf_op jit(solution)/shard_map/while/body/eval_jaxpr/cond/branch_0_fun/dot_general | solution.py:15
  377.5 5.2 fusion.21
  382.8 8.1 %broadcast_select_fusion.4 = (f32[64,2048]{1,0:T(8,128)S(1)}, f32[64,2048]{1,0:T(8,128)S(1)}) fusion(f32[64,2048]{1,0:T(8,128)S(1)} %fusion.21, pred[]{:T(512)S(6)} %lt.50, f32[64,1024]{1,0:T(8,128)S(1)} %get-tuple-element.396, f32[2048,1024]{1,0:T(8,128)S(1)} %get-tuple-element.410, f32[64,2048]{1,0:T(8,128)S(1)} %get-tuple-element.394, ...), kind=kOutput, calls=%fused_computation.52 | convolution fusion | flops 1611137024 | bytes 10756097 | tf_op jit(solution)/shard_map/while/body/eval_jaxpr/cond/branch_0_fun/dot_general | solution.py:29
  401.1 0.3 select_add_fusion.5
  405.4 0.7 dynamic_slice.87
  406.8 1.1 constant_dynamic-slice_fusion.5
  408.6 8.3 %dynamic-slice_bitcast_fusion.5 = f32[2048,1024]{1,0:T(8,128)} fusion(f32[2,2048,1024]{2,1,0:T(8,128)} %get-tuple-element.619, s32[]{:T(128)} %get-tuple-element.599), kind=kLoop, calls=%fused_computation.92.clone.1 | loop fusion | bytes 16777220 | tf_op jit(solution)/shard_map/while/body/jit(dynamic_index_in_dim)/squeeze | solution.py:130
  416.9 35.5 %conditional.7 = (f32[64,2048]{1,0:T(8,128)S(1)}, f32[64,2048]{1,0:T(8,128)S(1)}) conditional(s32[]{:T(128)} %convert_element_type.18, (s32[]{:T(128)}, s32[]{:T(128)}, f32[64,2048]{1,0:T(8,128)S(1)}, f32[64,2048]{1,0:T(8,128)S(1)}, f32[2048,1024]{1,0:T(8,128)}) %tuple.137, (f32[64,2048]{1,0:T(8,128)S(1)}, f32[2048,1024]{1,0:T(8,128)}) %tuple.110), branch_computations={%region_21.25_spmd, %region_26.34_spmd} | conditional | flops 7275405312 | bytes 84492352 | solution.py:88
  417.0 0.1 multiply_reduce_fusion.4
  417.1 12.0 %fusion.46 = (f32[1024]{0:T(1024)S(1)}, f32[2048]{0:T(1024)S(1)}, f32[2048,1024]{1,0:T(8,128)S(1)}) fusion(f32[2048,1024]{1,0:T(8,128)} %get-tuple-element.246, f32[64,2048]{1,0:T(8,128)S(1)} %get-tuple-element.394, f32[64,1024]{1,0:T(8,128)S(1)} %get-tuple-element.396, f32[1024]{0:T(1024)S(1)} %get-tuple-element.395, f32[2048]{0:T(1024)S(1)} %get-tuple-element.393), kind=kOutput, calls=%fused_computation.106 | convolution fusion | flops 1625289728 | bytes 17588224 | tf_op jit(solution)/shard_map/while/body/eval_jaxpr/cond/branch_0_fun/dot_general | solution.py:15
  429.1 5.2 fusion.21
  434.3 8.1 %broadcast_select_fusion.4 = (f32[64,2048]{1,0:T(8,128)S(1)}, f32[64,2048]{1,0:T(8,128)S(1)}) fusion(f32[64,2048]{1,0:T(8,128)S(1)} %fusion.21, pred[]{:T(512)S(6)} %lt.50, f32[64,1024]{1,0:T(8,128)S(1)} %get-tuple-element.396, f32[2048,1024]{1,0:T(8,128)S(1)} %get-tuple-element.410, f32[64,2048]{1,0:T(8,128)S(1)} %get-tuple-element.394, ...), kind=kOutput, calls=%fused_computation.52 | convolution fusion | flops 1611137024 | bytes 10756097 | tf_op jit(solution)/shard_map/while/body/eval_jaxpr/cond/branch_0_fun/dot_general | solution.py:29
  452.4 0.3 select_add_fusion.5
  457.9 0.8 copy-done.2
  458.7 0.0 all-reduce.17.cloned.1.call-start
  458.7 44.8 %all-reduce.15.cloned.1.call-done = f32[64,2048]{1,0:T(8,128)} async-done(((f32[64,2048]{1,0:T(8,128)}), f32[64,2048]{1,0:T(8,128)}) %all-reduce.15.cloned.1.call-update) | async-done | bytes 524304 | tf_op jit(solution)/shard_map/psum | solution.py:131
  503.6 0.1 add_dynamic-update-slice_fusion
  503.7 1.0 copy-done.4
  504.7 81.0 %all-reduce.17.cloned.1.call-done = f32[64,4096]{1,0:T(8,128)} async-done(((f32[64,4096]{1,0:T(8,128)}), f32[64,4096]{1,0:T(8,128)}) %all-reduce.17.cloned.1.call-update) | async-done | bytes 1048592 | tf_op jit(solution)/shard_map/psum | solution.py:136
  585.8 1.6 dynamic-slice_multiply_fusion
  (31 shorter events, 0.5 us)
Async XLA Ops:
  6.5 42.3 %all-gather.2.cloned.1.call-start = ((), (), s32[]{:S(2)}) async-start(), calls=%async_computation | async-start | bytes 1179648 | tf_op jit(solution)/shard_map/all_gather | solution.py:112
  7.3 77.3 %all-reduce.7.cloned.1.call-start = ((), (), s32[]{:S(2)}) async-start(), calls=%async_computation.1 | async-start | bytes 1048576 | tf_op jit(solution)/shard_map/psum | solution.py:11
  50.7 184.0 %all-reduce.9.cloned.1.call-start = ((), (), s32[]{:S(2)}) async-start(), calls=%async_computation.2 | async-start | bytes 1048576 | tf_op jit(solution)/shard_map/psum | solution.py:131
  88.0 8.3 %copy-start.1 = (f32[64,2048]{1,0:T(8,128)S(1)}, f32[64,2048]{1,0:T(8,128)}, u32[]{:S(2)}) copy-start(f32[64,2048]{1,0:T(8,128)} %get-tuple-element.581) | copy-start | bytes 1572868 | tf_op jit(solution)/shard_map/while
  139.3 8.3 %copy-start.1 = (f32[64,2048]{1,0:T(8,128)S(1)}, f32[64,2048]{1,0:T(8,128)}, u32[]{:S(2)}) copy-start(f32[64,2048]{1,0:T(8,128)} %get-tuple-element.581) | copy-start | bytes 1572868 | tf_op jit(solution)/shard_map/while
  189.0 0.8 copy-start.3
  189.8 126.9 %all-reduce.11.cloned.1.call-start = ((), (), s32[]{:S(2)}) async-start(), calls=%async_computation.3 | async-start | bytes 2097152 | tf_op jit(solution)/shard_map/psum | solution.py:136
  234.8 1.0 copy-start.5
  235.8 118.0 %all-reduce.13.cloned.1.call-start = ((), (), s32[]{:S(2)}) async-start(), calls=%async_computation.4 | async-start | bytes 1048576 | tf_op jit(solution)/shard_map/psum | solution.py:11
  321.0 182.6 %all-reduce.15.cloned.1.call-start = ((), (), s32[]{:S(2)}) async-start(), calls=%async_computation.5 | async-start | bytes 1048576 | tf_op jit(solution)/shard_map/psum | solution.py:131
  357.3 8.3 %copy-start = (f32[64,2048]{1,0:T(8,128)S(1)}, f32[64,2048]{1,0:T(8,128)}, u32[]{:S(2)}) copy-start(f32[64,2048]{1,0:T(8,128)} %get-tuple-element.620) | copy-start | bytes 1572868 | tf_op jit(solution)/shard_map/while
  408.6 8.3 %copy-start = (f32[64,2048]{1,0:T(8,128)S(1)}, f32[64,2048]{1,0:T(8,128)}, u32[]{:S(2)}) copy-start(f32[64,2048]{1,0:T(8,128)} %get-tuple-element.620) | copy-start | bytes 1572868 | tf_op jit(solution)/shard_map/while
  457.8 0.8 copy-start.2
  458.7 127.1 %all-reduce.17.cloned.1.call-start = ((), (), s32[]{:S(2)}) async-start(), calls=%async_computation.6 | async-start | bytes 2097152 | tf_op jit(solution)/shard_map/psum | solution.py:136
  503.7 1.0 copy-start.4
Sparse Core Ops, SparseCore 0:
  9.5 39.2 all-gather.1
  51.2 33.3 all-reduce.6
  189.9 44.7 all-reduce.8
  238.0 78.6 all-reduce.10
  321.1 32.6 all-reduce.12
  458.8 44.7 all-reduce.14
  507.1 78.6 all-reduce.16
where the time goes:
time: 598 us; the launch traced here: 595 us
  waiting for transfers between devices  360 us (60%)
  matrix products  101 us (17%)
  loops' own time  65.2 us (11%)
  local copies, waits for them, and re-layouts  44.3 us (7%)
  between operations  14 us (2%)
  other arithmetic  9.44 us (2%)
    psum x2, waiting for transfers between devices, local(): rows_coords = lax.psum(row_part, 'col') * inverse_count  162 us
    psum x2, waiting for transfers between devices, local(): col_total = lax.psum(col_part, 'row')  89.7 us
    psum x2, waiting for transfers between devices, from_root(): return lax.psum(kept, axis)  66.6 us
    dot_general x4, matrix products, compute_ratios(): lax.dot_general(leading, trailing, (((0,), (0,)), ((), ())), precision=la...  47.6 us
    all_gather x1, waiting for transfers between devices, local(): rows_coords = lax.all_gather(coords, 'col', axis=1, tiled=True)  41.5 us
    another operation x4, loops' own time, tile_terms(): lax.cond(row_index == col_index, diagonal_terms, offdiagonal_terms, value...  40.3 us
    squeeze x4, local copies, waits for them, and re-layouts, local(): lax.scan(one_tile, initial, (stacked_tiles, slot_indices))  33.3 us
    dot_general x4, matrix products, pair_terms(): lax.dot_general(trailing, ratios, (((1,), (1,)), ((), ())), precision=lax...  32.6 us
  transfers between devices with their start and end apart: 7, of which 7 were waited for; matrix products, arithmetic and copies ran while one was open for 0% of the time, Pallas kernels for 0%

commit v1 on v0

v1 whole, which is shorter than its diff:
```python
import functools

import jax
import jax.numpy as jnp
from jax import lax
from jax.experimental import pallas as pl
from jax.experimental.pallas import tpu as pltpu
from jax.sharding import PartitionSpec as P

ITERS = 2
STEP_ROWS = 512


def from_root(value, axis, source):
    kept = jnp.where(lax.axis_index(axis) == source, value, 0).astype(value.dtype)
    return lax.psum(kept, axis)


def terms_kernel(
    per_root, tile_count, x_ref, delta_ref, out_ref,
    lead_ref, pull_ref, trail_ref, push_ref, norm_col, norm_row, xt_ref, acc_t, acc,
):
    half = delta_ref.shape[1]
    block = 2 * half
    dims, count = x_ref.shape
    rows = delta_ref.shape[0]
    cols_at = tile_count * block
    step = pl.program_id(0)
    row_pos = lax.axis_index("row")
    col_pos = lax.axis_index("col")
    bf16, f32 = jnp.bfloat16, jnp.float32
    piece = 512

    @pl.when(step == 0)
    def _prepare():
        @pl.loop(0, count // piece)
        def _(k):
            at = pl.ds(pl.multiple_of(k * piece, piece), piece)
            x = x_ref[:, at]
            hi = x.astype(bf16).astype(f32)
            lo = (x - hi).astype(bf16).astype(f32)
            kept = hi + lo
            norm_row[:, at] = jnp.broadcast_to(
                jnp.sum(kept * kept, axis=0, keepdims=True), (8, piece)
            )
            stack = jnp.concatenate([hi, lo], axis=0)
            trail_ref[:, at] = jnp.concatenate([hi, hi, lo, lo], axis=0).astype(bf16) * -2.0
            push_ref[:, at] = jnp.concatenate(
                [hi, lo, jnp.ones((16, piece), f32)], axis=0
            ).astype(bf16)
            flipped = stack.T
            xt = flipped[:, :dims] + flipped[:, dims:]
            xt_ref[at, :] = xt
            norm_col[at, :] = jnp.sum(xt * xt, axis=1, keepdims=True) + 1.0
            pieces = flipped.astype(bf16)
            lead_ref[at, :] = jnp.concatenate([pieces, pieces], axis=1)
            pull_ref[at, :] = jnp.concatenate([pieces, jnp.ones_like(pieces)], axis=1)
            acc_t[at, :] = jnp.zeros((piece, dims), f32)
            acc[:, at] = jnp.zeros((dims, piece), f32)

    def spacing(lead, trail):
        gram = jnp.dot(lead_ref[lead, :], trail_ref[:, trail], preferred_element_type=f32)
        return gram + (norm_col[lead, :] + norm_row[0:1, trail])

    def add_terms(lead, trail, ratios):
        ratios = ratios.astype(bf16)
        pulled = jnp.dot(ratios, pull_ref[trail, :], preferred_element_type=f32)
        acc_t[lead, :] += xt_ref[lead, :] * pulled[:, 2 * dims:3 * dims] - (
            pulled[:, :dims] + pulled[:, dims:2 * dims]
        )
        pushed = jnp.dot(push_ref[:, lead], ratios, preferred_element_type=f32)
        acc[:, trail] += x_ref[:, trail] * pushed[2 * dims:2 * dims + 1, :] - (
            pushed[:dims, :] + pushed[dims:2 * dims, :]
        )

    steps_per_tile = block // rows
    slot = step // steps_per_tile
    first = (step % steps_per_tile) * rows
    row_index = row_pos * per_root + slot
    upper = (row_index == col_pos) & (first < half)
    slot_at = slot * block

    @pl.when(jnp.logical_not(upper))
    def _plain():
        lead_at = jnp.where(row_index > col_pos, cols_at, slot_at) + first
        trail_at = jnp.where(
            row_index < col_pos, cols_at,
            jnp.where(row_index > col_pos, slot_at + half, slot_at),
        )
        lead = pl.ds(pl.multiple_of(lead_at, rows), rows)
        trail = pl.ds(pl.multiple_of(trail_at, half), half)
        add_terms(lead, trail, delta_ref[...] * lax.rsqrt(spacing(lead, trail)))

    @pl.when(upper)
    def _split():
        early_lead = pl.ds(pl.multiple_of(slot_at + first, rows), rows)
        early_trail = pl.ds(pl.multiple_of(slot_at, half), half)
        late_lead = pl.ds(pl.multiple_of(slot_at + half + first, rows), rows)
        late_trail = pl.ds(pl.multiple_of(slot_at + half, half), half)
        row_iota = first + lax.broadcasted_iota(jnp.int32, (rows, half), 0)
        col_iota = lax.broadcasted_iota(jnp.int32, (rows, half), 1)
        early = jnp.where(
            col_iota > row_iota,
            delta_ref[...] * lax.rsqrt(spacing(early_lead, early_trail)), 0.0,
        )
        add_terms(early_lead, early_trail, early)
        late = jnp.where(
            col_iota < row_iota,
            delta_ref[...] * lax.rsqrt(spacing(late_lead, late_trail)), 0.0,
        )
        add_terms(late_lead, late_trail, late)

    @pl.when(step == pl.num_programs(0) - 1)
    def _finish():
        @pl.loop(0, count // piece)
        def _(k):
            at = pl.ds(pl.multiple_of(k * piece, piece), piece)
            out_ref[:, at] = acc[:, at] + acc_t[at, :].T


def local_terms(x, dissimilarity, per_root):
    dims, count = x.shape
    height, half = dissimilarity.shape
    tile_count = height // (2 * half)
    bf16, f32 = jnp.bfloat16, jnp.float32
    whole = pl.BlockSpec(memory_space=pltpu.VMEM)
    return pl.pallas_call(
        functools.partial(terms_kernel, per_root, tile_count),
        grid=(height // STEP_ROWS,),
        out_shape=jax.ShapeDtypeStruct((dims, count), f32),
        in_specs=[whole, pl.BlockSpec((STEP_ROWS, half), lambda i: (i, 0))],
        out_specs=whole,
        scratch_shapes=[
            pltpu.VMEM((count, 4 * dims), bf16),
            pltpu.VMEM((count, 4 * dims), bf16),
            pltpu.VMEM((4 * dims, count), bf16),
            pltpu.VMEM((2 * dims + 16, count), bf16),
            pltpu.VMEM((count, 1), f32),
            pltpu.VMEM((8, count), f32),
            pltpu.VMEM((count, dims), f32),
            pltpu.VMEM((count, dims), f32),
            pltpu.VMEM((dims, count), f32),
        ],
        compiler_params=pltpu.CompilerParams(vmem_limit_bytes=56 * 1024 * 1024),
    )(x, dissimilarity)


def local(coords, dissimilarity):
    half_width = dissimilarity.shape[1]
    block_width = 2 * half_width
    per_root = lax.axis_size("col") // lax.axis_size("row")
    inverse_count = 1.0 / (block_width * lax.axis_size("col"))
    row_pos = lax.axis_index("row")
    col_pos = lax.axis_index("col")
    own_width = coords.shape[1]
    column_offset = col_pos % per_root * block_width
    at_root = row_pos == col_pos // per_root
    current = coords
    for iteration in range(ITERS):
        rows_coords = lax.all_gather(current, "col", axis=1, tiled=True)
        height = rows_coords.shape[1]
        root_piece = lax.dynamic_slice_in_dim(rows_coords, column_offset, block_width, 1)
        cols_coords = from_root(root_piece, "row", col_pos // per_root)
        both = jnp.concatenate([rows_coords, cols_coords], axis=1)
        parts = local_terms(both, dissimilarity, per_root)
        row_part, col_part = parts[:, :height], parts[:, height:]
        col_total = lax.psum(col_part, "row")
        placed = lax.dynamic_update_slice_in_dim(
            jnp.zeros_like(row_part), col_total, column_offset, 1
        )
        row_part = row_part + jnp.where(at_root, placed, 0.0)
        current = lax.psum_scatter(row_part, "col", scatter_dimension=1, tiled=True) * inverse_count
    return current


def solution(mesh):
    in_specs = (P(None, ("row", "col")), P("row", "col"))
    out_specs = P(None, ("row", "col"))
    return jax.shard_map(local, mesh=mesh, in_specs=in_specs, out_specs=out_specs, check_vma=False)
```

time: 598 us -> 422 us (0.71)
  matrix products: 101 us -> 0 us
  loops' own time: 65.2 us -> 0 us
  local copies, waits for them, and re-layouts: 44.3 us -> 5.72 us
  Pallas kernels: 0 us -> 37.4 us
  waiting for transfers between devices: 360 us -> 351 us
    psum x2 -> x0, waiting for transfers between devices: 162 us -> none  [local(): rows_coords = lax.psum(row_part, 'col') * inverse_count]
    reduce_scatter x0 -> x2, waiting for transfers between devices: none -> 135 us  [local(): lax.psum_scatter(row_part, 'col', scatter_dimension=1, tiled=True)]
    dot_general x12 -> x0, matrix products: 101 us -> none  [the longest x4 47.6 us: compute_ratios(): lax.dot_general(leading, trailing, (((0,), (0,)), ((), ())), precision=la...]
    another operation x6 -> x0, loops' own time: 65.2 us -> none  [the longest x4 40.3 us: tile_terms(): lax.cond(row_index == col_index, diagonal_terms, offdiagonal_terms, value...]
    all_gather x1 -> x2, waiting for transfers between devices: 41.5 us -> 79.3 us  [local(): rows_coords = lax.all_gather(current, 'col', axis=1, tiled=True)]
    pallas_call x0 -> x2, Pallas kernels: none -> 37.4 us  [local_terms(): pl.pallas_call(functools.partial(terms_kernel, per_root, tile_count), gri...]
    squeeze x4 -> x0, local copies, waits for them, and re-layouts: 33.3 us -> none  [local(): lax.scan(one_tile, initial, (stacked_tiles, slot_indices))]
    psum x2, waiting for transfers between devices: 89.7 us -> 68.7 us  [local(): col_total = lax.psum(col_part, 'row')]
  transfers between devices with their start and end apart: 7 -> 8, of which waited for: 7 -> 8; matrix products, arithmetic and copies ran while one was open for 0% -> 0% of each run, Pallas kernels for 0% -> 0%
where the time goes in v1:
time: 422 us; the launch traced here: 420 us
  waiting for transfers between devices  351 us (83%)
  Pallas kernels  37.4 us (9%)
  between operations  13.6 us (3%)
  other arithmetic  11.9 us (3%)
  local copies, waits for them, and re-layouts  5.72 us (1%)
    reduce_scatter x2, waiting for transfers between devices, local(): lax.psum_scatter(row_part, 'col', scatter_dimension=1, tiled=True)  135 us
    all_gather x2, waiting for transfers between devices, local(): rows_coords = lax.all_gather(current, 'col', axis=1, tiled=True)  79.3 us
    psum x2, waiting for transfers between devices, local(): col_total = lax.psum(col_part, 'row')  68.7 us
    psum x2, waiting for transfers between devices, from_root(): return lax.psum(kept, axis)  67.3 us
    pallas_call x2, Pallas kernels, local_terms(): pl.pallas_call(functools.partial(terms_kernel, per_root, tile_count), gri...  37.4 us
  transfers between devices with their start and end apart: 8, of which 8 were waited for; matrix products, arithmetic and copies ran while one was open for 0% of the time, Pallas kernels for 0%

profile of v1, /device:TPU:14, one launch (start us, length us, event | category | flops | bytes accessed | tf_op | source)
XLA Modules:
  0.0 419.8 jit_solution(11359903832944313816)
XLA Ops:
  6.5 0.0 all-gather.3.cloned.1.call-start
  6.5 0.7 all-gather.3.cloned.1.call-update
  7.3 0.0 all-reduce.5.cloned.1.call-start
  7.3 41.5 %all-gather.3.cloned.1.call-done = f32[64,4096]{1,0:T(8,128)} async-done(((f32[64,512]{1,0:T(8,128)}), f32[64,4096]{1,0:T(8,128)}) %all-gather.3.cloned.1.call-update) | async-done | bytes 1048592 | tf_op jit(solution)/shard_map/all_gather | solution.py:160
  48.8 0.0 copy-start.2
  48.8 2.0 dynamic-slice_select_fusion.1
  50.8 0.0 all-reduce.5.cloned.1.call-update
  50.8 0.0 all-reduce.7.cloned.1.call-start
  50.9 33.7 %all-reduce.5.cloned.1.call-done = f32[64,2048]{1,0:T(8,128)} async-done(((f32[64,2048]{1,0:T(8,128)}), f32[64,2048]{1,0:T(8,128)}) %all-reduce.5.cloned.1.call-update) | async-done | bytes 524304 | tf_op jit(solution)/shard_map/psum | solution.py:16
  84.6 0.0 copy-done.2
  84.6 2.3 pad_maximum_fusion.x_ref
  86.9 18.7 %shard_map.28 = f32[64,6144]{1,0:T(8,128)} custom-call(f32[64,6144]{1,0:T(8,128)} %pad_maximum_fusion.x_ref, f32[4096,1024]{1,0:T(8,128)} %delta_ref.3), custom_call_target="tpu_custom_call" | custom-call | tf_op jit(solution)/shard_map/pallas_call | solution.py:127
  105.6 1.9 slice.23
  107.5 0.0 slice-start.1
  107.5 0.0 all-reduce.7.cloned.1.call-update
  107.5 0.0 reduce-scatter.3.cloned.1.call-start
  107.6 34.3 %all-reduce.7.cloned.1.call-done = f32[64,2048]{1,0:T(8,128)} async-done(((f32[64,2048]{1,0:T(8,128)}), f32[64,2048]{1,0:T(8,128)}) %all-reduce.7.cloned.1.call-update) | async-done | bytes 524304 | tf_op jit(solution)/shard_map/psum | solution.py:167
  141.9 0.0 slice-done.1
  141.9 0.1 add_dynamic-update-slice_fusion.1
  142.0 0.0 copy-start.1
  142.0 1.0 copy-done.1
  143.0 0.0 reduce-scatter.3.cloned.1.call-update
  143.0 0.0 all-gather.5.cloned.1.call-start
  143.0 67.4 %reduce-scatter.3.cloned.1.call-done = f32[64,512]{1,0:T(8,128)} async-done(((f32[64,4096]{1,0:T(8,128)}), f32[64,512]{1,0:T(8,128)}) %reduce-scatter.3.cloned.1.call-update) | async-done | bytes 131088 | tf_op jit(solution)/shard_map/reduce_scatter | solution.py:172
  210.4 1.6 broadcast_multiply_fusion.1
  212.0 0.0 all-gather.5.cloned.1.call-update
  212.0 0.0 all-reduce.9.cloned.1.call-start
  212.1 37.8 %all-gather.5.cloned.1.call-done = f32[64,4096]{1,0:T(8,128)} async-done(((f32[64,512]{1,0:T(8,128)}), f32[64,4096]{1,0:T(8,128)}) %all-gather.5.cloned.1.call-update) | async-done | bytes 1048592 | tf_op jit(solution)/shard_map/all_gather | solution.py:160
  249.8 0.0 copy-start.3
  249.8 2.0 dynamic-slice_select_fusion
  251.8 0.0 all-reduce.9.cloned.1.call-update
  251.8 0.0 all-reduce.11.cloned.1.call-start
  251.9 33.6 %all-reduce.9.cloned.1.call-done = f32[64,2048]{1,0:T(8,128)} async-done(((f32[64,2048]{1,0:T(8,128)}), f32[64,2048]{1,0:T(8,128)}) %all-reduce.9.cloned.1.call-update) | async-done | bytes 524304 | tf_op jit(solution)/shard_map/psum | solution.py:16
  285.4 0.0 copy-done.3
  285.4 2.3 pad_maximum_fusion.1.x_ref
  287.7 18.7 %shard_map.29 = f32[64,6144]{1,0:T(8,128)} custom-call(f32[64,6144]{1,0:T(8,128)} %pad_maximum_fusion.1.x_ref, f32[4096,1024]{1,0:T(8,128)} %delta_ref.3), custom_call_target="tpu_custom_call" | custom-call | tf_op jit(solution)/shard_map/pallas_call | solution.py:127
  306.5 1.9 slice.25
  308.3 0.0 slice-start
  308.3 0.0 all-reduce.11.cloned.1.call-update
  308.4 0.0 reduce-scatter.5.cloned.1.call-start
  308.4 34.4 %all-reduce.11.cloned.1.call-done = f32[64,2048]{1,0:T(8,128)} async-done(((f32[64,2048]{1,0:T(8,128)}), f32[64,2048]{1,0:T(8,128)}) %all-reduce.11.cloned.1.call-update) | async-done | bytes 524304 | tf_op jit(solution)/shard_map/psum | solution.py:167
  342.8 0.0 slice-done
  342.8 0.1 add_dynamic-update-slice_fusion
  342.9 0.0 copy-start
  342.9 1.0 copy-done
  343.9 0.0 reduce-scatter.5.cloned.1.call-update
  343.9 67.5 %reduce-scatter.5.cloned.1.call-done = f32[64,512]{1,0:T(8,128)} async-done(((f32[64,4096]{1,0:T(8,128)}), f32[64,512]{1,0:T(8,128)}) %reduce-scatter.5.cloned.1.call-update) | async-done | bytes 131088 | tf_op jit(solution)/shard_map/reduce_scatter | solution.py:172
  411.4 1.6 broadcast_multiply_fusion
Async XLA Ops:
  6.5 42.3 %all-gather.3.cloned.1.call-start = ((), (), s32[]{:S(2)}) async-start(), calls=%async_computation.2 | async-start | bytes 1179648 | tf_op jit(solution)/shard_map/all_gather | solution.py:160
  7.3 77.3 %all-reduce.5.cloned.1.call-start = ((), (), s32[]{:S(2)}) async-start(), calls=%async_computation.3 | async-start | bytes 1048576 | tf_op jit(solution)/shard_map/psum | solution.py:16
  48.8 35.8 %copy-start.2 = (f32[64,4096]{1,0:T(8,128)S(1)}, f32[64,4096]{1,0:T(8,128)}, u32[]{:S(2)}) copy-start(f32[64,4096]{1,0:T(8,128)} %all-gather.3.cloned.1.call-done) | copy-start | bytes 3145732
  50.8 91.1 %all-reduce.7.cloned.1.call-start = ((), (), s32[]{:S(2)}) async-start(), calls=%async_computation.4 | async-start | bytes 1048576 | tf_op jit(solution)/shard_map/psum | solution.py:167
  107.5 34.4 %slice-start.1 = ((f32[64,6144]{1,0:T(8,128)}), f32[64,4096]{1,0:T(8,128)S(1)}, s32[]{:S(2)}) async-start(f32[64,6144]{1,0:T(8,128)} %shard_map.28), calls=%async_computation.11 | async-start | bytes 2097152 | tf_op jit(solution)/shard_map/slice | solution.py:166
  107.5 102.9 %reduce-scatter.3.cloned.1.call-start = ((), (), s32[]{:S(2)}) async-start(), calls=%async_computation.5 | async-start | bytes 1179648 | tf_op jit(solution)/shard_map/reduce_scatter | solution.py:172
  142.0 1.0 copy-start.1
  143.0 106.8 %all-gather.5.cloned.1.call-start = ((), (), s32[]{:S(2)}) async-start(), calls=%async_computation.6 | async-start | bytes 1179648 | tf_op jit(solution)/shard_map/all_gather | solution.py:160
  212.0 73.4 %all-reduce.9.cloned.1.call-start = ((), (), s32[]{:S(2)}) async-start(), calls=%async_computation.7 | async-start | bytes 1048576 | tf_op jit(solution)/shard_map/psum | solution.py:16
  249.8 35.6 %copy-start.3 = (f32[64,4096]{1,0:T(8,128)S(1)}, f32[64,4096]{1,0:T(8,128)}, u32[]{:S(2)}) copy-start(f32[64,4096]{1,0:T(8,128)} %all-gather.5.cloned.1.call-done) | copy-start | bytes 3145732
  251.8 90.9 %all-reduce.11.cloned.1.call-start = ((), (), s32[]{:S(2)}) async-start(), calls=%async_computation.8 | async-start | bytes 1048576 | tf_op jit(solution)/shard_map/psum | solution.py:167
  308.3 34.4 %slice-start = ((f32[64,6144]{1,0:T(8,128)}), f32[64,4096]{1,0:T(8,128)S(1)}, s32[]{:S(2)}) async-start(f32[64,6144]{1,0:T(8,128)} %shard_map.29), calls=%async_computation.10 | async-start | bytes 2097152 | tf_op jit(solution)/shard_map/slice | solution.py:166
  308.4 103.1 %reduce-scatter.5.cloned.1.call-start = ((), (), s32[]{:S(2)}) async-start(), calls=%async_computation.9 | async-start | bytes 1179648 | tf_op jit(solution)/shard_map/reduce_scatter | solution.py:172
  342.9 1.0 copy-start
Sparse Core Ops, SparseCore 0:
  9.5 39.2 all-gather.2
  51.2 33.3 all-reduce.4
  107.6 34.2 all-reduce.6
  145.1 65.2 reduce-scatter.2
  212.5 37.3 all-gather.4
  252.0 33.3 all-reduce.8
  308.5 34.2 all-reduce.10
  346.2 65.2 reduce-scatter.4

commit v2 on v1

--- a/solution.py
+++ b/solution.py
@@ -9,11 +9,6 @@
 
 ITERS = 2
 STEP_ROWS = 512
-
-
-def from_root(value, axis, source):
-    kept = jnp.where(lax.axis_index(axis) == source, value, 0).astype(value.dtype)
-    return lax.psum(kept, axis)
 
 
 def terms_kernel(
@@ -145,32 +140,274 @@
     )(x, dissimilarity)
 
 
-def local(coords, dissimilarity):
-    half_width = dissimilarity.shape[1]
-    block_width = 2 * half_width
-    per_root = lax.axis_size("col") // lax.axis_size("row")
-    inverse_count = 1.0 / (block_width * lax.axis_size("col"))
+def exchange_kernel(scatter, gather, n_row, n_col, slow, fast, width, inverse, *refs):
+    refs = list(refs)
+    in_ref, out_ref = refs[0], refs[1]
+    if scatter:
+        (work, own, core_buf, sum_buf, row_buf, x_buf, up_buf, down_buf,
+         core_s, core_r, row_s, row_r, x_s, x_r, up_s, up_r, down_s, down_r) = refs[2:20]
+        refs = refs[20:]
+    else:
+        refs = refs[2:]
+    if gather:
+        gup_s, gup_r, gdown_s, gdown_r, gx_s, gx_r, grow_s, gcore_s, gcol_r = refs
+    per_root = n_col // n_row
+    per_block = n_col // per_root
+    height = n_col * width
     row_pos = lax.axis_index("row")
     col_pos = lax.axis_index("col")
-    own_width = coords.shape[1]
-    column_offset = col_pos % per_root * block_width
-    at_root = row_pos == col_pos // per_root
-    current = coords
+    z, x = col_pos // fast, col_pos % fast
+    which = col_pos % per_root
+    root = col_pos // per_root
+    at_root = row_pos == root
+    same_core = row_pos % 2 == root % 2
+    relays = same_core & (row_pos != root)
+    groups = n_row // 2
+    group, core = row_pos // 2, row_pos % 2
+    has_up, has_down = z < slow - 1, z > 0
+    above, below = {"col": (z + 1) * fast + x}, {"col": (z - 1) * fast + x}
+    core_peer = {"row": group * 2 + 1 - core}
+    sent = []
+
+    def beside(e):
+        return {"col": z * fast + (x + e) % fast}
+
+    def when(pred, body):
+        if pred is True:
+            body()
+        else:
+            pl.when(pred)(body)
+
+    def send(pred, make):
+        when(pred, lambda: make().start())
+        sent.append((pred, make))
+
+    def remote(src, dst, send_sem, recv_sem, peer):
+        return pltpu.make_async_remote_copy(
+            src_ref=src, dst_ref=dst, send_sem=send_sem, recv_sem=recv_sem,
+            device_id=peer, device_id_type=pl.DeviceIdType.MESH,
+        )
+
+    def arrived(dst, recv_sem):
+        remote(dst, dst, recv_sem, recv_sem, core_peer).wait_recv()
+
+    def chunk(zz, xx):
+        return pl.ds(pl.multiple_of((zz * fast + xx) * width, width), width)
+
+    def column(kk):
+        return pl.ds(pl.multiple_of(height + kk * width, width), width)
+
+    barrier = pltpu.get_barrier_semaphore()
+
+    def greet(peer):
+        pl.semaphore_signal(barrier, inc=1, device_id=peer, device_id_type=pl.DeviceIdType.MESH)
+
+    when(has_up, lambda: greet(above))
+    when(has_down, lambda: greet(below))
+    for e in range(1, fast):
+        greet(beside(e))
+    for g in range(1, groups):
+        greet({"row": (group + g) % groups * 2 + core})
+    greet(core_peer)
+    neighbours = jnp.where(has_up, 1, 0) + jnp.where(has_down, 1, 0)
+    pl.semaphore_wait(barrier, fast - 1 + groups + neighbours)
+
+    if scatter:
+        for kk in range(per_block):
+            send(jnp.logical_not(same_core), lambda kk=kk: remote(
+                in_ref.at[:, column(kk)], core_buf.at[kk], core_s.at[kk], core_r.at[kk], core_peer))
+        work[...] = in_ref[:, :height]
+        shift = (which + 1) * per_block // fast % slow
+        for k in range(slow):
+            zz = (k + shift) % slow
+
+            def settle(zz=zz):
+                for xx in range(fast):
+                    kk = zz * fast + xx - which * per_block
+                    arrived(core_buf.at[kk], core_r.at[kk])
+                    total = work[:, chunk(zz, xx)] + in_ref[:, column(kk)] + core_buf[kk]
+                    for g in range(1, groups):
+                        other = (group + g) % groups
+                        arrived(row_buf.at[other, kk], row_r.at[other, kk])
+                        total += row_buf[other, kk]
+                    work[:, chunk(zz, xx)] = total
+
+            when(at_root & (zz * fast // per_block == which), settle)
+            for e in range(1, fast):
+                send(True, lambda zz=zz, e=e: remote(
+                    work.at[:, chunk(zz, (x + e) % fast)], x_buf.at[e - 1, zz],
+                    x_s.at[e - 1, zz], x_r.at[e - 1, zz], beside(e)))
+        for kk in range(per_block):
+            def relay_sum(kk=kk):
+                arrived(core_buf.at[kk], core_r.at[kk])
+                sum_buf[kk] = in_ref[:, column(kk)] + core_buf[kk]
+            when(relays, relay_sum)
+            send(relays, lambda kk=kk: remote(
+                sum_buf.at[kk], row_buf.at[group, kk], row_s.at[kk], row_r.at[group, kk], {"row": root}))
+
+        def across(zz):
+            total = work[:, chunk(zz, x)]
+            for e in range(1, fast):
+                arrived(x_buf.at[e - 1, zz], x_r.at[e - 1, zz])
+                total += x_buf[e - 1, zz]
+            return total
+
+        def pass_on(zz, has_behind, buf, recv):
+            total = across(zz)
+            work[:, chunk(zz, x)] = total
+
+            @pl.when(has_behind)
+            def _():
+                arrived(buf.at[zz], recv.at[zz])
+                work[:, chunk(zz, x)] += buf[zz]
+
+        for d in range(slow - 1, 0, -1):
+            when(z + d < slow, lambda d=d: pass_on(z + d, has_down, up_buf, up_r))
+            send(z + d < slow, lambda d=d: remote(
+                work.at[:, chunk(z + d, x)], up_buf.at[z + d], up_s.at[z + d], up_r.at[z + d], above))
+            when(z - d >= 0, lambda d=d: pass_on(z - d, has_up, down_buf, down_r))
+            send(z - d >= 0, lambda d=d: remote(
+                work.at[:, chunk(z - d, x)], down_buf.at[z - d], down_s.at[z - d], down_r.at[z - d], below))
+        own[...] = across(z)
+
+        @pl.when(has_down)
+        def _():
+            arrived(up_buf.at[z], up_r.at[z])
+            own[...] += up_buf[z]
+
+        @pl.when(has_up)
+        def _():
+            arrived(down_buf.at[z], down_r.at[z])
+            own[...] += down_buf[z]
+
+        mine = own[...] * inverse
+    else:
+        mine = in_ref[...]
+
+    if gather:
+        out_ref[:, chunk(z, x)] = mine
+
+        def hand_on(zz, pred, upward, downward):
+            there = out_ref.at[:, chunk(zz, x)]
+            if upward is not None:
+                send(upward, lambda: remote(there, there, gup_s.at[zz], gup_r.at[zz], above))
+            if downward is not None:
+                send(downward, lambda: remote(there, there, gdown_s.at[zz], gdown_r.at[zz], below))
+            for e in range(1, fast):
+                send(pred, lambda e=e: remote(
+                    there, there, gx_s.at[e - 1, zz], gx_r.at[e - 1, zz], beside(e)))
+
+        def to_column(zz, xx, pred):
+            kk = zz * fast + xx - which * per_block
+            wanted = at_root & ((zz * fast + xx) // per_block == which)
+            if pred is not True:
+                wanted = wanted & pred
+
+            def place():
+                out_ref[:, column(kk)] = out_ref[:, chunk(zz, xx)]
+
+            for g in range(1, groups):
+                send(wanted, lambda g=g: remote(
+                    out_ref.at[:, chunk(zz, xx)], out_ref.at[:, column(kk)],
+                    grow_s.at[g - 1, kk], gcol_r.at[kk], {"row": (group + g) % groups * 2 + core}))
+            send(wanted, lambda: remote(
+                out_ref.at[:, chunk(zz, xx)], out_ref.at[:, column(kk)],
+                gcore_s.at[kk], gcol_r.at[kk], core_peer))
+            when(wanted, place)
+
+        def from_beside(zz, pred):
+            for e in range(1, fast):
+                xx = (x + fast - e) % fast
+                when(pred, lambda: arrived(out_ref.at[:, chunk(zz, xx)], gx_r.at[e - 1, zz]))
+                to_column(zz, xx, pred)
+
+        hand_on(z, True, has_up, has_down)
+        to_column(z, x, True)
+        for d in range(1, slow):
+            low, high = z - d, z + d
+            when(low >= 0, lambda: arrived(out_ref.at[:, chunk(low, x)], gup_r.at[low]))
+            hand_on(low, low >= 0, (low >= 0) & has_up, None)
+            to_column(low, x, low >= 0)
+            when(high < slow, lambda: arrived(out_ref.at[:, chunk(high, x)], gdown_r.at[high]))
+            hand_on(high, high < slow, None, (high < slow) & has_down)
+            to_column(high, x, high < slow)
+            if d == 1:
+                from_beside(z, True)
+            else:
+                from_beside(low + 1, low + 1 >= 0)
+                from_beside(high - 1, high - 1 < slow)
+        from_beside(z - slow + 1, z - slow + 1 >= 0)
+        from_beside(z + slow - 1, z + slow - 1 < slow)
+        for kk in range(per_block):
+            when(jnp.logical_not(at_root), lambda: arrived(out_ref.at[:, column(kk)], gcol_r.at[kk]))
+            send(relays, lambda kk=kk: remote(
+                out_ref.at[:, column(kk)], out_ref.at[:, column(kk)],
+                gcore_s.at[kk], gcol_r.at[kk], core_peer))
+    else:
+        out_ref[...] = mine
+    for pred, make in sent:
+        when(pred, lambda: make().wait_send())
+
+
+def exchange(value, scatter, gather, n_row, n_col, width, inverse, collective_id):
+    fast = 1
+    while fast * fast * 4 <= n_col:
+        fast *= 2
+    slow = n_col // fast
+    per_block = n_row
+    dims = value.shape[0]
+    f32 = jnp.float32
+    dma = pltpu.SemaphoreType.DMA
+    total = (n_col + per_block) * width
+    scratch = []
+    if scatter:
+        piece = (dims, width)
+        groups = n_row // 2
+        scratch += [
+            pltpu.VMEM((dims, n_col * width), f32),
+            pltpu.VMEM(piece, f32),
+            pltpu.VMEM((per_block,) + piece, f32),
+            pltpu.VMEM((per_block,) + piece, f32),
+            pltpu.VMEM((groups, per_block) + piece, f32),
+            pltpu.VMEM((fast - 1, slow) + piece, f32),
+            pltpu.VMEM((slow,) + piece, f32),
+            pltpu.VMEM((slow,) + piece, f32),
+            dma((per_block,)), dma((per_block,)), dma((per_block,)), dma((groups, per_block)),
+            dma((fast - 1, slow)), dma((fast - 1, slow)),
+            dma((slow,)), dma((slow,)), dma((slow,)), dma((slow,)),
+        ]
+    if gather:
+        scratch += [
+            dma((slow,)), dma((slow,)), dma((slow,)), dma((slow,)),
+            dma((fast - 1, slow)), dma((fast - 1, slow)),
+            dma((max(n_row // 2 - 1, 1), per_block)), dma((per_block,)), dma((per_block,)),
+        ]
+    whole = pl.BlockSpec(memory_space=pltpu.VMEM)
+    return pl.pallas_call(
+        functools.partial(
+            exchange_kernel, scatter, gather, n_row, n_col, slow, fast, width, inverse
+        ),
+        out_shape=jax.ShapeDtypeStruct((dims, total if gather else width), f32),
+        in_specs=[whole],
+        out_specs=whole,
+        scratch_shapes=scratch,
+        compiler_params=pltpu.CompilerParams(
+            collective_id=collective_id, has_side_effects=True, vmem_limit_bytes=48 * 1024 * 1024
+        ),
+    )(value)
+
+
+def local(coords, dissimilarity):
+    n_row, n_col = lax.axis_size("row"), lax.axis_size("col")
+    width = coords.shape[1]
+    inverse = 1.0 / (width * n_row * n_col)
+    trade = functools.partial(exchange, n_row=n_row, n_col=n_col, width=width, inverse=inverse)
+    both = trade(coords, False, True, collective_id=0)
     for iteration in range(ITERS):
-        rows_coords = lax.all_gather(current, "col", axis=1, tiled=True)
-        height = rows_coords.shape[1]
-        root_piece = lax.dynamic_slice_in_dim(rows_coords, column_offset, block_width, 1)
-        cols_coords = from_root(root_piece, "row", col_pos // per_root)
-        both = jnp.concatenate([rows_coords, cols_coords], axis=1)
-        parts = local_terms(both, dissimilarity, per_root)
-        row_part, col_part = parts[:, :height], parts[:, height:]
-        col_total = lax.psum(col_part, "row")
-        placed = lax.dynamic_update_slice_in_dim(
-            jnp.zeros_like(row_part), col_total, column_offset, 1
-        )
-        row_part = row_part + jnp.where(at_root, placed, 0.0)
-        current = lax.psum_scatter(row_part, "col", scatter_dimension=1, tiled=True) * inverse_count
-    return current
+        parts = local_terms(both, dissimilarity, n_col // n_row)
+        last = iteration == ITERS - 1
+        both = trade(parts, True, not last, collective_id=1 + iteration)
+    return both
 
 
 def solution(mesh):

time: 422 us -> 150 us (0.36)
  the two profiles are of different devices: /device:TPU:14 before, /device:TPU:8 now
where the time goes in v2:
time: 150 us; the launch traced here: 149 us
  Pallas kernels  143 us (95%)
  local copies, waits for them, and re-layouts  6.69 us (4%)
    pallas_call x3, Pallas kernels, exchange(): pl.pallas_call(functools.partial(exchange_kernel, scatter, gather, n_row,...  105 us
    pallas_call x2, Pallas kernels, local_terms(): pl.pallas_call(functools.partial(terms_kernel, per_root, tile_count), gri...  37.4 us
    unnamed x11, local copies, waits for them, and re-layouts  6.69 us

profile of v2, /device:TPU:8, one launch (start us, length us, event | category | flops | bytes accessed | tf_op | source)
XLA Modules:
  0.0 149.3 jit_solution(17550105113918984005)
XLA Ops:
  0.0 0.0 copy-start.4
  0.0 0.9 copy-done.4
  0.9 15.7 %shard_map.28.x_ref = f32[64,6144]{1,0:T(8,128)S(1)} custom-call(f32[64,512]{1,0:T(8,128)S(1)} %copy-done.4), custom_call_target="tpu_custom_call" | custom-call | tf_op jit(solution)/shard_map/pallas_call | solution.py:386
  16.6 0.0 copy-start.3
  16.6 1.2 copy-done.3
  17.8 18.7 %shard_map.29.refs_0_ = f32[64,6144]{1,0:T(8,128)} custom-call(f32[64,6144]{1,0:T(8,128)} %copy-done.3, f32[4096,1024]{1,0:T(8,128)} %delta_ref.3), custom_call_target="tpu_custom_call" | custom-call | tf_op jit(solution)/shard_map/pallas_call | solution.py:122
  36.5 0.0 copy-start
  36.5 1.4 copy-done
  37.9 49.4 %shard_map.30.x_ref = f32[64,6144]{1,0:T(8,128)S(1)} custom-call(f32[64,6144]{1,0:T(8,128)S(1)} %copy-done), custom_call_target="tpu_custom_call" | custom-call | tf_op jit(solution)/shard_map/pallas_call | solution.py:386
  87.3 0.0 copy-start.1
  87.3 1.2 copy-done.1
  88.5 18.7 %shard_map.31.refs_0_ = f32[64,6144]{1,0:T(8,128)} custom-call(f32[64,6144]{1,0:T(8,128)} %copy-done.1, f32[4096,1024]{1,0:T(8,128)} %delta_ref.3), custom_call_target="tpu_custom_call" | custom-call | tf_op jit(solution)/shard_map/pallas_call | solution.py:122
  107.2 0.0 copy-start.2
  107.2 1.4 copy-done.2
  108.6 40.0 %shard_map.32 = f32[64,512]{1,0:T(8,128)S(1)} custom-call(f32[64,6144]{1,0:T(8,128)S(1)} %copy-done.2), custom_call_target="tpu_custom_call" | custom-call | tf_op jit(solution)/shard_map/pallas_call | solution.py:386
  148.7 0.7 copy.4
Async XLA Ops:
  0.0 0.9 copy-start.4
  16.6 1.2 copy-start.3
  36.5 1.4 copy-start
  87.3 1.2 copy-start.1
  107.2 1.4 copy-start.2

commit v3 on v2

--- a/solution.py
+++ b/solution.py
@@ -13,7 +13,7 @@
 
 def terms_kernel(
     per_root, tile_count, x_ref, delta_ref, out_ref,
-    lead_ref, pull_ref, trail_ref, push_ref, norm_col, norm_row, xt_ref, acc_t, acc,
+    lead_ref, trail_ref, push_ref, norm_col, norm_row,
 ):
     half = delta_ref.shape[1]
     block = 2 * half
@@ -35,38 +35,31 @@
             hi = x.astype(bf16).astype(f32)
             lo = (x - hi).astype(bf16).astype(f32)
             kept = hi + lo
-            norm_row[:, at] = jnp.broadcast_to(
-                jnp.sum(kept * kept, axis=0, keepdims=True), (8, piece)
-            )
-            stack = jnp.concatenate([hi, lo], axis=0)
+            norms = jnp.sum(kept * kept, axis=0, keepdims=True)
+            norm_row[:, at] = jnp.broadcast_to(norms, (8, piece))
+            norm_col[at, :] = jnp.broadcast_to(norms + 1.0, (128, piece)).T
             trail_ref[:, at] = jnp.concatenate([hi, hi, lo, lo], axis=0).astype(bf16) * -2.0
-            push_ref[:, at] = jnp.concatenate(
-                [hi, lo, jnp.ones((16, piece), f32)], axis=0
-            ).astype(bf16)
+            stack = jnp.concatenate([hi, lo], axis=0).astype(bf16)
+            push_ref[:, at] = jnp.concatenate([stack, jnp.ones((16, piece), bf16)], axis=0)
             flipped = stack.T
-            xt = flipped[:, :dims] + flipped[:, dims:]
-            xt_ref[at, :] = xt
-            norm_col[at, :] = jnp.sum(xt * xt, axis=1, keepdims=True) + 1.0
-            pieces = flipped.astype(bf16)
-            lead_ref[at, :] = jnp.concatenate([pieces, pieces], axis=1)
-            pull_ref[at, :] = jnp.concatenate([pieces, jnp.ones_like(pieces)], axis=1)
-            acc_t[at, :] = jnp.zeros((piece, dims), f32)
-            acc[:, at] = jnp.zeros((dims, piece), f32)
+            lead_ref[at, :] = jnp.concatenate([flipped, flipped], axis=1)
+            out_ref[:, at] = jnp.zeros((dims, piece), f32)
 
     def spacing(lead, trail):
         gram = jnp.dot(lead_ref[lead, :], trail_ref[:, trail], preferred_element_type=f32)
-        return gram + (norm_col[lead, :] + norm_row[0:1, trail])
+        wide = jnp.concatenate([norm_col[lead, :]] * (half // 128), axis=1)
+        return gram + (wide + norm_row[0:1, trail])
 
     def add_terms(lead, trail, ratios):
         ratios = ratios.astype(bf16)
-        pulled = jnp.dot(ratios, pull_ref[trail, :], preferred_element_type=f32)
-        acc_t[lead, :] += xt_ref[lead, :] * pulled[:, 2 * dims:3 * dims] - (
-            pulled[:, :dims] + pulled[:, dims:2 * dims]
+        pulled = lax.dot_general(
+            push_ref[:, trail], ratios, (((1,), (1,)), ((), ())), preferred_element_type=f32
         )
         pushed = jnp.dot(push_ref[:, lead], ratios, preferred_element_type=f32)
-        acc[:, trail] += x_ref[:, trail] * pushed[2 * dims:2 * dims + 1, :] - (
-            pushed[:dims, :] + pushed[dims:2 * dims, :]
-        )
+        for at, moved in ((lead, pulled), (trail, pushed)):
+            out_ref[:, at] += x_ref[:, at] * moved[2 * dims:2 * dims + 1, :] - (
+                moved[:dims, :] + moved[dims:2 * dims, :]
+            )
 
     steps_per_tile = block // rows
     slot = step // steps_per_tile
@@ -105,13 +98,6 @@
         )
         add_terms(late_lead, late_trail, late)
 
-    @pl.when(step == pl.num_programs(0) - 1)
-    def _finish():
-        @pl.loop(0, count // piece)
-        def _(k):
-            at = pl.ds(pl.multiple_of(k * piece, piece), piece)
-            out_ref[:, at] = acc[:, at] + acc_t[at, :].T
-
 
 def local_terms(x, dissimilarity, per_root):
     dims, count = x.shape
@@ -127,14 +113,10 @@
         out_specs=whole,
         scratch_shapes=[
             pltpu.VMEM((count, 4 * dims), bf16),
-            pltpu.VMEM((count, 4 * dims), bf16),
             pltpu.VMEM((4 * dims, count), bf16),
             pltpu.VMEM((2 * dims + 16, count), bf16),
-            pltpu.VMEM((count, 1), f32),
+            pltpu.VMEM((count, 128), f32),
             pltpu.VMEM((8, count), f32),
-            pltpu.VMEM((count, dims), f32),
-            pltpu.VMEM((count, dims), f32),
-            pltpu.VMEM((dims, count), f32),
         ],
         compiler_params=pltpu.CompilerParams(vmem_limit_bytes=56 * 1024 * 1024),
     )(x, dissimilarity)
@@ -145,8 +127,8 @@
     in_ref, out_ref = refs[0], refs[1]
     if scatter:
         (work, own, core_buf, sum_buf, row_buf, x_buf, up_buf, down_buf,
-         core_s, core_r, row_s, row_r, x_s, x_r, up_s, up_r, down_s, down_r) = refs[2:20]
-        refs = refs[20:]
+         late_buf, late_s, late_r, core_s, core_r, row_s, row_r, x_s, x_r, up_s, up_r, down_s, down_r) = refs[2:23]
+        refs = refs[23:]
     else:
         refs = refs[2:]
     if gather:
@@ -210,32 +192,26 @@
         greet({"row": (group + g) % groups * 2 + core})
     greet(core_peer)
     neighbours = jnp.where(has_up, 1, 0) + jnp.where(has_down, 1, 0)
+    my_root = row_pos * per_root + col_pos // per_block
+    if scatter:
+        when(my_root != col_pos, lambda: greet({"col": my_root}))
+        neighbours += jnp.where(my_root != col_pos, 1, 0)
+        for kk in range(per_block):
+            owned = at_root & (which * per_block + kk != col_pos)
+            when(owned, lambda: greet({"col": which * per_block + kk}))
+            neighbours += jnp.where(owned, 1, 0)
     pl.semaphore_wait(barrier, fast - 1 + groups + neighbours)
 
     if scatter:
         for kk in range(per_block):
             send(jnp.logical_not(same_core), lambda kk=kk: remote(
                 in_ref.at[:, column(kk)], core_buf.at[kk], core_s.at[kk], core_r.at[kk], core_peer))
-        work[...] = in_ref[:, :height]
-        shift = (which + 1) * per_block // fast % slow
-        for k in range(slow):
-            zz = (k + shift) % slow
-
-            def settle(zz=zz):
-                for xx in range(fast):
-                    kk = zz * fast + xx - which * per_block
-                    arrived(core_buf.at[kk], core_r.at[kk])
-                    total = work[:, chunk(zz, xx)] + in_ref[:, column(kk)] + core_buf[kk]
-                    for g in range(1, groups):
-                        other = (group + g) % groups
-                        arrived(row_buf.at[other, kk], row_r.at[other, kk])
-                        total += row_buf[other, kk]
-                    work[:, chunk(zz, xx)] = total
-
-            when(at_root & (zz * fast // per_block == which), settle)
+        order = [z + d for d in range(slow - 1, 0, -1)] + [z - d for d in range(slow - 1, 0, -1)]
+        order = [order[i + h * (slow - 1)] for i in range(slow - 1) for h in range(2)] + [z]
+        for zz in order:
             for e in range(1, fast):
-                send(True, lambda zz=zz, e=e: remote(
-                    work.at[:, chunk(zz, (x + e) % fast)], x_buf.at[e - 1, zz],
+                send((zz >= 0) & (zz < slow), lambda zz=zz, e=e: remote(
+                    in_ref.at[:, chunk(zz, (x + e) % fast)], x_buf.at[e - 1, zz],
                     x_s.at[e - 1, zz], x_r.at[e - 1, zz], beside(e)))
         for kk in range(per_block):
             def relay_sum(kk=kk):
@@ -245,8 +221,17 @@
             send(relays, lambda kk=kk: remote(
                 sum_buf.at[kk], row_buf.at[group, kk], row_s.at[kk], row_r.at[group, kk], {"row": root}))
 
+        def settle(kk):
+            arrived(core_buf.at[kk], core_r.at[kk])
+            total = in_ref[:, column(kk)] + core_buf[kk]
+            for g in range(1, groups):
+                other = (group + g) % groups
+                arrived(row_buf.at[other, kk], row_r.at[other, kk])
+                total += row_buf[other, kk]
+            sum_buf[kk] = total
+
         def across(zz):
-            total = work[:, chunk(zz, x)]
+            total = in_ref[:, chunk(zz, x)]
             for e in range(1, fast):
                 arrived(x_buf.at[e - 1, zz], x_r.at[e - 1, zz])
                 total += x_buf[e - 1, zz]
@@ -268,6 +253,12 @@
             when(z - d >= 0, lambda d=d: pass_on(z - d, has_up, down_buf, down_r))
             send(z - d >= 0, lambda d=d: remote(
                 work.at[:, chunk(z - d, x)], down_buf.at[z - d], down_s.at[z - d], down_r.at[z - d], below))
+            for kk in range(per_block):
+                if kk * (slow - 1) // per_block == slow - 1 - d:
+                    when(at_root, lambda: settle(kk))
+                    send(at_root & (which * per_block + kk != col_pos), lambda kk=kk: remote(
+                        sum_buf.at[kk], late_buf, late_s.at[kk], late_r,
+                        {"col": which * per_block + kk}))
         own[...] = across(z)
 
         @pl.when(has_down)
@@ -279,6 +270,15 @@
         def _():
             arrived(down_buf.at[z], down_r.at[z])
             own[...] += down_buf[z]
+
+        @pl.when(my_root != col_pos)
+        def _():
+            arrived(late_buf, late_r)
+            own[...] += late_buf[...]
+
+        @pl.when(my_root == col_pos)
+        def _():
+            own[...] += sum_buf[col_pos % per_block]
 
         mine = own[...] * inverse
     else:
@@ -372,6 +372,7 @@
             pltpu.VMEM((fast - 1, slow) + piece, f32),
             pltpu.VMEM((slow,) + piece, f32),
             pltpu.VMEM((slow,) + piece, f32),
+            pltpu.VMEM(piece, f32), dma((per_block,)), dma,
             dma((per_block,)), dma((per_block,)), dma((per_block,)), dma((groups, per_block)),
             dma((fast - 1, slow)), dma((fast - 1, slow)),
             dma((slow,)), dma((slow,)), dma((slow,)), dma((slow,)),

time: 150 us -> 135 us (0.900)
  the two profiles are of different devices: /device:TPU:8 before, /device:TPU:14 now
where the time goes in v3:
time: 135 us; the launch traced here: 134 us
  Pallas kernels  128 us (95%)
  local copies, waits for them, and re-layouts  6.69 us (5%)
    pallas_call x3, Pallas kernels, exchange(): pl.pallas_call(functools.partial(exchange_kernel, scatter, gather, n_row,...  95.7 us
    pallas_call x2, Pallas kernels, local_terms(): pl.pallas_call(functools.partial(terms_kernel, per_root, tile_count), gri...  32.1 us
    unnamed x11, local copies, waits for them, and re-layouts  6.69 us

profile of v3, /device:TPU:14, one launch (start us, length us, event | category | flops | bytes accessed | tf_op | source)
XLA Modules:
  0.0 134.5 jit_solution(15728842570818026035)
XLA Ops:
  0.0 0.0 copy-start.4
  0.0 0.9 copy-done.4
  0.9 16.4 %shard_map.28.x_ref = f32[64,6144]{1,0:T(8,128)S(1)} custom-call(f32[64,512]{1,0:T(8,128)S(1)} %copy-done.4), custom_call_target="tpu_custom_call" | custom-call | tf_op jit(solution)/shard_map/pallas_call | solution.py:387
  17.4 0.0 copy-start.3
  17.4 1.2 copy-done.3
  18.5 16.0 %shard_map.29.refs_0_ = f32[64,6144]{1,0:T(8,128)} custom-call(f32[64,6144]{1,0:T(8,128)} %copy-done.3, f32[4096,1024]{1,0:T(8,128)} %delta_ref.3), custom_call_target="tpu_custom_call" | custom-call | tf_op jit(solution)/shard_map/pallas_call | solution.py:108
  34.6 0.0 copy-start
  34.6 1.4 %copy-done = f32[64,6144]{1,0:T(8,128)S(1)} copy-done((f32[64,6144]{1,0:T(8,128)S(1)}, f32[64,6144]{1,0:T(8,128)}, u32[]{:S(2)}) %copy-start) | copy-done | bytes 1572888
  36.0 47.1 %shard_map.30.x_ref = f32[64,6144]{1,0:T(8,128)S(1)} custom-call(f32[64,6144]{1,0:T(8,128)S(1)} %copy-done), custom_call_target="tpu_custom_call" | custom-call | tf_op jit(solution)/shard_map/pallas_call | solution.py:387
  83.0 0.0 copy-start.1
  83.0 1.2 copy-done.1
  84.2 16.0 %shard_map.31.refs_0_ = f32[64,6144]{1,0:T(8,128)} custom-call(f32[64,6144]{1,0:T(8,128)} %copy-done.1, f32[4096,1024]{1,0:T(8,128)} %delta_ref.3), custom_call_target="tpu_custom_call" | custom-call | tf_op jit(solution)/shard_map/pallas_call | solution.py:108
  100.2 0.0 copy-start.2
  100.2 1.4 %copy-done.2 = f32[64,6144]{1,0:T(8,128)S(1)} copy-done((f32[64,6144]{1,0:T(8,128)S(1)}, f32[64,6144]{1,0:T(8,128)}, u32[]{:S(2)}) %copy-start.2) | copy-done | bytes 1572888
  101.6 32.2 %shard_map.32 = f32[64,512]{1,0:T(8,128)S(1)} custom-call(f32[64,6144]{1,0:T(8,128)S(1)} %copy-done.2), custom_call_target="tpu_custom_call" | custom-call | tf_op jit(solution)/shard_map/pallas_call | solution.py:387
  133.8 0.7 copy.4
Async XLA Ops:
  0.0 0.9 copy-start.4
  17.4 1.2 copy-start.3
  34.6 1.4 %copy-start = (f32[64,6144]{1,0:T(8,128)S(1)}, f32[64,6144]{1,0:T(8,128)}, u32[]{:S(2)}) copy-start(f32[64,6144]{1,0:T(8,128)} %shard_map.29.refs_0_) | copy-start | bytes 4718596
  83.0 1.2 copy-start.1
  100.2 1.4 %copy-start.2 = (f32[64,6144]{1,0:T(8,128)S(1)}, f32[64,6144]{1,0:T(8,128)}, u32[]{:S(2)}) copy-start(f32[64,6144]{1,0:T(8,128)} %shard_map.31.refs_0_) | copy-start | bytes 4718596

commit v4 on v3

--- a/solution.py
+++ b/solution.py
@@ -9,6 +9,7 @@
 
 ITERS = 2
 STEP_ROWS = 512
+PARTS = 2
 
 
 def terms_kernel(
@@ -24,7 +25,7 @@
     row_pos = lax.axis_index("row")
     col_pos = lax.axis_index("col")
     bf16, f32 = jnp.bfloat16, jnp.float32
-    piece = 512
+    piece = 1024
 
     @pl.when(step == 0)
     def _prepare():
@@ -176,6 +177,10 @@
     def chunk(zz, xx):
         return pl.ds(pl.multiple_of((zz * fast + xx) * width, width), width)
 
+    def part(h):
+        size = out_ref.shape[0] // PARTS
+        return pl.ds(h * size, size)
+
     def column(kk):
         return pl.ds(pl.multiple_of(height + kk * width, width), width)
 
@@ -210,9 +215,10 @@
         order = [order[i + h * (slow - 1)] for i in range(slow - 1) for h in range(2)] + [z]
         for zz in order:
             for e in range(1, fast):
-                send((zz >= 0) & (zz < slow), lambda zz=zz, e=e: remote(
-                    in_ref.at[:, chunk(zz, (x + e) % fast)], x_buf.at[e - 1, zz],
-                    x_s.at[e - 1, zz], x_r.at[e - 1, zz], beside(e)))
+                for h in range(PARTS):
+                    send((zz >= 0) & (zz < slow), lambda zz=zz, e=e, h=h: remote(
+                        in_ref.at[part(h), chunk(zz, (x + e) % fast)], x_buf.at[e - 1, zz, part(h)],
+                        x_s.at[h, e - 1, zz], x_r.at[h, e - 1, zz], beside(e)))
         for kk in range(per_block):
             def relay_sum(kk=kk):
                 arrived(core_buf.at[kk], core_r.at[kk])
@@ -230,46 +236,45 @@
                 total += row_buf[other, kk]
             sum_buf[kk] = total
 
-        def across(zz):
-            total = in_ref[:, chunk(zz, x)]
+        def across(h, zz):
+            total = in_ref[part(h), chunk(zz, x)]
             for e in range(1, fast):
-                arrived(x_buf.at[e - 1, zz], x_r.at[e - 1, zz])
-                total += x_buf[e - 1, zz]
+                arrived(x_buf.at[e - 1, zz, part(h)], x_r.at[h, e - 1, zz])
+                total += x_buf[e - 1, zz, part(h)]
             return total
 
-        def pass_on(zz, has_behind, buf, recv):
-            total = across(zz)
-            work[:, chunk(zz, x)] = total
+        def pass_on(h, zz, has_behind, buf, recv):
+            work[part(h), chunk(zz, x)] = across(h, zz)
 
             @pl.when(has_behind)
             def _():
-                arrived(buf.at[zz], recv.at[zz])
-                work[:, chunk(zz, x)] += buf[zz]
+                arrived(buf.at[zz, part(h)], recv.at[h, zz])
+                work[part(h), chunk(zz, x)] += buf[zz, part(h)]
 
         for d in range(slow - 1, 0, -1):
-            when(z + d < slow, lambda d=d: pass_on(z + d, has_down, up_buf, up_r))
-            send(z + d < slow, lambda d=d: remote(
-                work.at[:, chunk(z + d, x)], up_buf.at[z + d], up_s.at[z + d], up_r.at[z + d], above))
-            when(z - d >= 0, lambda d=d: pass_on(z - d, has_up, down_buf, down_r))
-            send(z - d >= 0, lambda d=d: remote(
-                work.at[:, chunk(z - d, x)], down_buf.at[z - d], down_s.at[z - d], down_r.at[z - d], below))
+            for h in range(PARTS):
+                when(z + d < slow, lambda: pass_on(h, z + d, has_down, up_buf, up_r))
+                send(z + d < slow, lambda d=d, h=h: remote(
+                    work.at[part(h), chunk(z + d, x)], up_buf.at[z + d, part(h)],
+                    up_s.at[h, z + d], up_r.at[h, z + d], above))
+                when(z - d >= 0, lambda: pass_on(h, z - d, has_up, down_buf, down_r))
+                send(z - d >= 0, lambda d=d, h=h: remote(
+                    work.at[part(h), chunk(z - d, x)], down_buf.at[z - d, part(h)],
+                    down_s.at[h, z - d], down_r.at[h, z - d], below))
             for kk in range(per_block):
                 if kk * (slow - 1) // per_block == slow - 1 - d:
                     when(at_root, lambda: settle(kk))
                     send(at_root & (which * per_block + kk != col_pos), lambda kk=kk: remote(
                         sum_buf.at[kk], late_buf, late_s.at[kk], late_r,
                         {"col": which * per_block + kk}))
-        own[...] = across(z)
-
-        @pl.when(has_down)
-        def _():
-            arrived(up_buf.at[z], up_r.at[z])
-            own[...] += up_buf[z]
-
-        @pl.when(has_up)
-        def _():
-            arrived(down_buf.at[z], down_r.at[z])
-            own[...] += down_buf[z]
+        def close(h, buf, recv):
+            arrived(buf.at[z, part(h)], recv.at[h, z])
+            own[part(h), :] += buf[z, part(h)]
+
+        for h in range(PARTS):
+            own[part(h), :] = across(h, z)
+            when(has_down, lambda: close(h, up_buf, up_r))
+            when(has_up, lambda: close(h, down_buf, down_r))
 
         @pl.when(my_root != col_pos)
         def _():
@@ -287,62 +292,67 @@
     if gather:
         out_ref[:, chunk(z, x)] = mine
 
-        def hand_on(zz, pred, upward, downward):
-            there = out_ref.at[:, chunk(zz, x)]
+        def hand_on(h, zz, pred, upward, downward):
+            there = out_ref.at[part(h), chunk(zz, x)]
             if upward is not None:
-                send(upward, lambda: remote(there, there, gup_s.at[zz], gup_r.at[zz], above))
+                send(upward, lambda: remote(there, there, gup_s.at[h, zz], gup_r.at[h, zz], above))
             if downward is not None:
-                send(downward, lambda: remote(there, there, gdown_s.at[zz], gdown_r.at[zz], below))
+                send(downward, lambda: remote(there, there, gdown_s.at[h, zz], gdown_r.at[h, zz], below))
             for e in range(1, fast):
                 send(pred, lambda e=e: remote(
-                    there, there, gx_s.at[e - 1, zz], gx_r.at[e - 1, zz], beside(e)))
-
-        def to_column(zz, xx, pred):
+                    there, there, gx_s.at[h, e - 1, zz], gx_r.at[h, e - 1, zz], beside(e)))
+
+        def to_column(h, zz, xx, pred):
             kk = zz * fast + xx - which * per_block
             wanted = at_root & ((zz * fast + xx) // per_block == which)
             if pred is not True:
                 wanted = wanted & pred
 
             def place():
-                out_ref[:, column(kk)] = out_ref[:, chunk(zz, xx)]
+                out_ref[part(h), column(kk)] = out_ref[part(h), chunk(zz, xx)]
 
             for g in range(1, groups):
                 send(wanted, lambda g=g: remote(
-                    out_ref.at[:, chunk(zz, xx)], out_ref.at[:, column(kk)],
-                    grow_s.at[g - 1, kk], gcol_r.at[kk], {"row": (group + g) % groups * 2 + core}))
+                    out_ref.at[part(h), chunk(zz, xx)], out_ref.at[part(h), column(kk)],
+                    grow_s.at[h, g - 1, kk], gcol_r.at[h, kk], {"row": (group + g) % groups * 2 + core}))
             send(wanted, lambda: remote(
-                out_ref.at[:, chunk(zz, xx)], out_ref.at[:, column(kk)],
-                gcore_s.at[kk], gcol_r.at[kk], core_peer))
+                out_ref.at[part(h), chunk(zz, xx)], out_ref.at[part(h), column(kk)],
+                gcore_s.at[h, kk], gcol_r.at[h, kk], core_peer))
             when(wanted, place)
 
-        def from_beside(zz, pred):
+        def from_beside(h, zz, pred):
             for e in range(1, fast):
                 xx = (x + fast - e) % fast
-                when(pred, lambda: arrived(out_ref.at[:, chunk(zz, xx)], gx_r.at[e - 1, zz]))
-                to_column(zz, xx, pred)
-
-        hand_on(z, True, has_up, has_down)
-        to_column(z, x, True)
+                when(pred, lambda: arrived(out_ref.at[part(h), chunk(zz, xx)], gx_r.at[h, e - 1, zz]))
+                to_column(h, zz, xx, pred)
+
+        for h in range(PARTS):
+            hand_on(h, z, True, has_up, has_down)
+            to_column(h, z, x, True)
         for d in range(1, slow):
             low, high = z - d, z + d
-            when(low >= 0, lambda: arrived(out_ref.at[:, chunk(low, x)], gup_r.at[low]))
-            hand_on(low, low >= 0, (low >= 0) & has_up, None)
-            to_column(low, x, low >= 0)
-            when(high < slow, lambda: arrived(out_ref.at[:, chunk(high, x)], gdown_r.at[high]))
-            hand_on(high, high < slow, None, (high < slow) & has_down)
-            to_column(high, x, high < slow)
-            if d == 1:
-                from_beside(z, True)
-            else:
-                from_beside(low + 1, low + 1 >= 0)
-                from_beside(high - 1, high - 1 < slow)
-        from_beside(z - slow + 1, z - slow + 1 >= 0)
-        from_beside(z + slow - 1, z + slow - 1 < slow)
+            for h in range(PARTS):
+                when(low >= 0, lambda: arrived(out_ref.at[part(h), chunk(low, x)], gup_r.at[h, low]))
+                hand_on(h, low, low >= 0, (low >= 0) & has_up, None)
+                to_column(h, low, x, low >= 0)
+                when(high < slow, lambda: arrived(out_ref.at[part(h), chunk(high, x)], gdown_r.at[h, high]))
+                hand_on(h, high, high < slow, None, (high < slow) & has_down)
+                to_column(h, high, x, high < slow)
+                if d == 1:
+                    from_beside(h, z, True)
+                else:
+                    from_beside(h, low + 1, low + 1 >= 0)
+                    from_beside(h, high - 1, high - 1 < slow)
+        for h in range(PARTS):
+            from_beside(h, z - slow + 1, z - slow + 1 >= 0)
+            from_beside(h, z + slow - 1, z + slow - 1 < slow)
         for kk in range(per_block):
-            when(jnp.logical_not(at_root), lambda: arrived(out_ref.at[:, column(kk)], gcol_r.at[kk]))
-            send(relays, lambda kk=kk: remote(
-                out_ref.at[:, column(kk)], out_ref.at[:, column(kk)],
-                gcore_s.at[kk], gcol_r.at[kk], core_peer))
+            for h in range(PARTS):
+                when(jnp.logical_not(at_root), lambda: arrived(
+                    out_ref.at[part(h), column(kk)], gcol_r.at[h, kk]))
+                send(relays, lambda kk=kk, h=h: remote(
+                    out_ref.at[part(h), column(kk)], out_ref.at[part(h), column(kk)],
+                    gcore_s.at[h, kk], gcol_r.at[h, kk], core_peer))
     else:
         out_ref[...] = mine
     for pred, make in sent:
@@ -374,14 +384,14 @@
             pltpu.VMEM((slow,) + piece, f32),
             pltpu.VMEM(piece, f32), dma((per_block,)), dma,
             dma((per_block,)), dma((per_block,)), dma((per_block,)), dma((groups, per_block)),
-            dma((fast - 1, slow)), dma((fast - 1, slow)),
-            dma((slow,)), dma((slow,)), dma((slow,)), dma((slow,)),
+            dma((PARTS, fast - 1, slow)), dma((PARTS, fast - 1, slow)),
+            dma((PARTS, slow)), dma((PARTS, slow)), dma((PARTS, slow)), dma((PARTS, slow)),
         ]
     if gather:
         scratch += [
-            dma((slow,)), dma((slow,)), dma((slow,)), dma((slow,)),
-            dma((fast - 1, slow)), dma((fast - 1, slow)),
-            dma((max(n_row // 2 - 1, 1), per_block)), dma((per_block,)), dma((per_block,)),
+            dma((PARTS, slow)), dma((PARTS, slow)), dma((PARTS, slow)), dma((PARTS, slow)),
+            dma((PARTS, fast - 1, slow)), dma((PARTS, fast - 1, slow)),
+            dma((PARTS, max(n_row // 2 - 1, 1), per_block)), dma((PARTS, per_block)), dma((PARTS, per_block)),
         ]
     whole = pl.BlockSpec(memory_space=pltpu.VMEM)
     return pl.pallas_call(

time: 135 us -> 127 us (0.941)
  Pallas kernels: 128 us -> 120 us
    pallas_call x3, Pallas kernels: 95.7 us -> 89.4 us  [exchange(): pl.pallas_call(functools.partial(exchange_kernel, scatter, gather, n_row,...]
where the time goes in v4:
time: 127 us
  Pallas kernels  120 us (94%)
  local copies, waits for them, and re-layouts  6.69 us (5%)
    pallas_call x3, Pallas kernels, exchange(): pl.pallas_call(functools.partial(exchange_kernel, scatter, gather, n_row,...  89.4 us
    pallas_call x2, Pallas kernels, local_terms(): pl.pallas_call(functools.partial(terms_kernel, per_root, tile_count), gri...  30.9 us
    unnamed x11, local copies, waits for them, and re-layouts  6.69 us

profile of v4, /device:TPU:14, one launch (start us, length us, event | category | flops | bytes accessed | tf_op | source)
XLA Modules:
  0.0 127.1 jit_solution(1353917050162626080)
XLA Ops:
  0.0 0.0 copy-start.4
  0.0 0.9 copy-done.4
  0.9 16.2 %shard_map.28.x_ref = f32[64,6144]{1,0:T(8,128)S(1)} custom-call(f32[64,512]{1,0:T(8,128)S(1)} %copy-done.4), custom_call_target="tpu_custom_call" | custom-call | tf_op jit(solution)/shard_map/pallas_call | solution.py:397
  17.1 0.0 copy-start.3
  17.1 1.2 copy-done.3
  18.3 15.5 %shard_map.29.refs_0_ = f32[64,6144]{1,0:T(8,128)} custom-call(f32[64,6144]{1,0:T(8,128)} %copy-done.3, f32[4096,1024]{1,0:T(8,128)} %delta_ref.3), custom_call_target="tpu_custom_call" | custom-call | tf_op jit(solution)/shard_map/pallas_call | solution.py:109
  33.8 0.0 copy-start
  33.8 1.4 %copy-done = f32[64,6144]{1,0:T(8,128)S(1)} copy-done((f32[64,6144]{1,0:T(8,128)S(1)}, f32[64,6144]{1,0:T(8,128)}, u32[]{:S(2)}) %copy-start) | copy-done | bytes 1572888
  35.2 43.8 %shard_map.30.x_ref = f32[64,6144]{1,0:T(8,128)S(1)} custom-call(f32[64,6144]{1,0:T(8,128)S(1)} %copy-done), custom_call_target="tpu_custom_call" | custom-call | tf_op jit(solution)/shard_map/pallas_call | solution.py:397
  79.0 0.0 copy-start.1
  79.0 1.2 copy-done.1
  80.2 15.5 %shard_map.31.refs_0_ = f32[64,6144]{1,0:T(8,128)} custom-call(f32[64,6144]{1,0:T(8,128)} %copy-done.1, f32[4096,1024]{1,0:T(8,128)} %delta_ref.3), custom_call_target="tpu_custom_call" | custom-call | tf_op jit(solution)/shard_map/pallas_call | solution.py:109
  95.6 0.0 copy-start.2
  95.6 1.4 %copy-done.2 = f32[64,6144]{1,0:T(8,128)S(1)} copy-done((f32[64,6144]{1,0:T(8,128)S(1)}, f32[64,6144]{1,0:T(8,128)}, u32[]{:S(2)}) %copy-start.2) | copy-done | bytes 1572888
  97.0 29.4 %shard_map.32 = f32[64,512]{1,0:T(8,128)S(1)} custom-call(f32[64,6144]{1,0:T(8,128)S(1)} %copy-done.2), custom_call_target="tpu_custom_call" | custom-call | tf_op jit(solution)/shard_map/pallas_call | solution.py:397
  126.4 0.7 copy.4
Async XLA Ops:
  0.0 0.9 copy-start.4
  17.1 1.2 copy-start.3
  33.8 1.4 %copy-start = (f32[64,6144]{1,0:T(8,128)S(1)}, f32[64,6144]{1,0:T(8,128)}, u32[]{:S(2)}) copy-start(f32[64,6144]{1,0:T(8,128)} %shard_map.29.refs_0_) | copy-start | bytes 4718596
  79.0 1.2 copy-start.1
  95.6 1.4 %copy-start.2 = (f32[64,6144]{1,0:T(8,128)S(1)}, f32[64,6144]{1,0:T(8,128)}, u32[]{:S(2)}) copy-start(f32[64,6144]{1,0:T(8,128)} %shard_map.31.refs_0_) | copy-start | bytes 4718596

commit v5 on v4

--- a/solution.py
+++ b/solution.py
@@ -9,7 +9,7 @@
 
 ITERS = 2
 STEP_ROWS = 512
-PARTS = 2
+PARTS = 4
 
 
 def terms_kernel(

time: 127 us -> 130 us (1.024)
  Pallas kernels: 120 us -> 122 us
    pallas_call x3, Pallas kernels: 89.4 us -> 91.6 us  [exchange(): pl.pallas_call(functools.partial(exchange_kernel, scatter, gather, n_row,...]
where the time goes in v5:
time: 130 us; the launch traced here: 129 us
  Pallas kernels  122 us (94%)
  local copies, waits for them, and re-layouts  6.69 us (5%)
    pallas_call x3, Pallas kernels, exchange(): pl.pallas_call(functools.partial(exchange_kernel, scatter, gather, n_row,...  91.6 us
    pallas_call x2, Pallas kernels, local_terms(): pl.pallas_call(functools.partial(terms_kernel, per_root, tile_count), gri...  30.9 us
    unnamed x11, local copies, waits for them, and re-layouts  6.69 us

profile of v5, /device:TPU:14, one launch (start us, length us, event | category | flops | bytes accessed | tf_op | source)
XLA Modules:
  0.0 129.2 jit_solution(11723228786681586356)
XLA Ops:
  0.0 0.0 copy-start.4
  0.0 0.9 copy-done.4
  0.9 16.8 %shard_map.28.x_ref = f32[64,6144]{1,0:T(8,128)S(1)} custom-call(f32[64,512]{1,0:T(8,128)S(1)} %copy-done.4), custom_call_target="tpu_custom_call" | custom-call | tf_op jit(solution)/shard_map/pallas_call | solution.py:397
  17.7 0.0 copy-start.3
  17.7 1.2 copy-done.3
  18.9 15.5 %shard_map.29.refs_0_ = f32[64,6144]{1,0:T(8,128)} custom-call(f32[64,6144]{1,0:T(8,128)} %copy-done.3, f32[4096,1024]{1,0:T(8,128)} %delta_ref.3), custom_call_target="tpu_custom_call" | custom-call | tf_op jit(solution)/shard_map/pallas_call | solution.py:109
  34.3 0.0 copy-start
  34.3 1.4 %copy-done = f32[64,6144]{1,0:T(8,128)S(1)} copy-done((f32[64,6144]{1,0:T(8,128)S(1)}, f32[64,6144]{1,0:T(8,128)}, u32[]{:S(2)}) %copy-start) | copy-done | bytes 1572888
  35.7 46.0 %shard_map.30.x_ref = f32[64,6144]{1,0:T(8,128)S(1)} custom-call(f32[64,6144]{1,0:T(8,128)S(1)} %copy-done), custom_call_target="tpu_custom_call" | custom-call | tf_op jit(solution)/shard_map/pallas_call | solution.py:397
  81.7 0.0 copy-start.1
  81.8 1.2 copy-done.1
  82.9 15.5 %shard_map.31.refs_0_ = f32[64,6144]{1,0:T(8,128)} custom-call(f32[64,6144]{1,0:T(8,128)} %copy-done.1, f32[4096,1024]{1,0:T(8,128)} %delta_ref.3), custom_call_target="tpu_custom_call" | custom-call | tf_op jit(solution)/shard_map/pallas_call | solution.py:109
  98.4 0.0 copy-start.2
  98.4 1.4 %copy-done.2 = f32[64,6144]{1,0:T(8,128)S(1)} copy-done((f32[64,6144]{1,0:T(8,128)S(1)}, f32[64,6144]{1,0:T(8,128)}, u32[]{:S(2)}) %copy-start.2) | copy-done | bytes 1572888
  99.8 28.8 %shard_map.32 = f32[64,512]{1,0:T(8,128)S(1)} custom-call(f32[64,6144]{1,0:T(8,128)S(1)} %copy-done.2), custom_call_target="tpu_custom_call" | custom-call | tf_op jit(solution)/shard_map/pallas_call | solution.py:397
  128.6 0.7 copy.4
Async XLA Ops:
  0.0 0.9 copy-start.4
  17.7 1.2 copy-start.3
  34.3 1.4 %copy-start = (f32[64,6144]{1,0:T(8,128)S(1)}, f32[64,6144]{1,0:T(8,128)}, u32[]{:S(2)}) copy-start(f32[64,6144]{1,0:T(8,128)} %shard_map.29.refs_0_) | copy-start | bytes 4718596
  81.7 1.2 copy-start.1
  98.4 1.4 %copy-start.2 = (f32[64,6144]{1,0:T(8,128)S(1)}, f32[64,6144]{1,0:T(8,128)}, u32[]{:S(2)}) copy-start(f32[64,6144]{1,0:T(8,128)} %shard_map.31.refs_0_) | copy-start | bytes 4718596
